TPU v7x, 256 devices: a whole 4x4x8 slice. The times are simulated.
256 devices in a mesh: depth: 8 (over y, core), rays: 32 (over z, x).
Axes of the slice: x: 4, y: 4, z: 8, core: 2. Of those that a mesh axis runs over, the one named last changes fastest.
Arguments:
- encodings: bfloat16 [8, 163840, 8, 128], P('depth', 'rays'), may hold values from -6 to 6
- spacing: float32 [8, 8, 163840], P('depth', None, 'rays'), may hold values from 0.01 to 0.1
- ray_ids: int32 [8, 163840], P('depth', 'rays'), may hold values from 0 to 8191, as said below
- live_count: int32 [8, 32], P('depth', 'rays'), may hold values from 1280 to 5120, as said below
- pixel_of_ray: int32 [262144], P('rays'), may hold values from 0 to 262143, as said below
- w_first: bfloat16 [8, 128, 128], P('depth'), may hold values from -0.5 to 0.5
- b_first: float32 [8, 128], P('depth'), may hold values from -3 to 3
- w_second: bfloat16 [8, 128, 128], P('depth'), may hold values from -0.5 to 0.5
- b_second: float32 [8, 128], P('depth'), may hold values from -3 to 3
- w_density: bfloat16 [8, 128], P('depth'), may hold values from -0.5 to 0.5
- w_feature: bfloat16 [8, 128, 128], P('depth'), may hold values from -1.5 to 1.5
- kernel_one: bfloat16 [5, 5, 128, 128], replicated, may hold values from -0.109375 to 0.109375
- bias_one: float32 [128], replicated, may hold values from -2 to 2
- kernel_two: bfloat16 [5, 5, 128, 128], replicated, may hold values from -0.109375 to 0.109375
- bias_two: float32 [128], replicated, may hold values from -2 to 2
Outputs:
- rendered: bfloat16 [512, 512, 128], P('rays', 'depth')
Inputs may be any that keep to these rules, and one draw needn't show every extreme that they name: `ray_ids`: within the 5120 slots of one partition and bundle the ray ids are distinct; only the first live_count slots are live. `live_count`: some partition and bundle has all 5120 slots live. `pixel_of_ray`: A permutation of the image's pixels. Split the image into blocks of 16 rows by 64 columns: every bundle's 8192 rays hold exactly 32 pixels of every block.
All inputs are finite; a program needn't handle non-finite values.
Results may differ from a plain program's by a relative error of at most 0.013.
Values may be sent and summed in bfloat16 or wider, within the bound.
No kernel may reach another device: no remote copies, remote signals or barrier semaphores. Data moves between devices by JAX's collectives and lax.ppermute only.
A program may use at most 128 MiB of HBM per device.

v0:
```python
import jax
import jax.numpy as jnp
from jax import lax
from jax.sharding import PartitionSpec as P

FEAT = 128
TH = 16
TW = 64


def padded_2(array, sides, width):
    for axis, dim in sides:
        size, length = (lax.axis_size(axis), array.shape[dim])
        up = [(i, (i + 1) % size) for i in range(size - 1)]
        down = [(j, i) for i, j in up]
        last = lax.slice_in_dim(array, length - width, length, axis=dim)
        first = lax.slice_in_dim(array, 0, width, axis=dim)
        before = lax.ppermute(last, axis, up)
        after = lax.ppermute(first, axis, down)
        array = jnp.concatenate([before, array, after], axis=dim)
    return array


def entering(array, axis, join, neutral):
    place = lax.axis_index(axis)
    gathered = lax.all_gather(array.astype(jnp.bfloat16), axis)
    state = jnp.zeros_like(array) + jnp.asarray(neutral, array.dtype)

    def one(hop, state):
        return join(state, lax.dynamic_index_in_dim(gathered, hop, 0, False).astype(array.dtype))

    return lax.fori_loop(0, place, one, state)


def slot_terms(encoded, spacing_block, ray_index, live_total, weights, colour_base, depth_base):
    w_first, b_first, w_second, b_second, w_density, w_feature = weights
    slot_total, samples, enc_width = encoded.shape
    flat_rows = encoded.reshape(slot_total * samples, enc_width)
    hidden_one = jnp.maximum(
        jnp.dot(flat_rows, w_first, preferred_element_type=jnp.float32) + b_first, 0.0
    ).astype(jnp.bfloat16)
    hidden_two = jnp.maximum(
        jnp.dot(hidden_one, w_second, preferred_element_type=jnp.float32) + b_second, 0.0
    ).astype(jnp.bfloat16)
    density = jax.nn.softplus(
        jnp.dot(hidden_two, w_density, preferred_element_type=jnp.float32)
    ).reshape(slot_total, samples)
    feature = jnp.dot(hidden_two, w_feature, preferred_element_type=jnp.float32).reshape(
        slot_total, samples, -1
    )
    opacity = density * spacing_block
    within = jnp.cumsum(opacity, axis=1) - opacity
    weight = jnp.exp(-within) * (1.0 - jnp.exp(-opacity))
    colour = jnp.einsum("ns,nsf->nf", weight, feature)
    live_mask = (jnp.arange(slot_total) < live_total).astype(jnp.float32)
    colour_out = colour_base.at[ray_index].add(colour * live_mask[:, None])
    depth_out = depth_base.at[ray_index].add(jnp.sum(opacity, axis=1) * live_mask)
    return (colour_out, depth_out)


def group_slots(group_of_ray, group_count):
    ray_total = group_of_ray.shape[0]
    per_group = ray_total // group_count
    member = (group_of_ray[:, None] == jnp.arange(group_count, dtype=jnp.int32)[None, :]).astype(
        jnp.int32
    )
    running = jnp.cumsum(member, axis=0)
    rank_in_group = jnp.sum(running * member, axis=1) - 1
    return group_of_ray * per_group + rank_in_group


def convolve(block_in, kernel, bias):
    reach = kernel.shape[0] // 2
    padded = padded_2(block_in, (("depth", 1), ("rays", 0)), reach)
    rows_here, cols_here, channels = block_in.shape
    windows = jnp.concatenate(
        [
            padded[row_off : row_off + rows_here, col_off : col_off + cols_here]
            for row_off in range(kernel.shape[0])
            for col_off in range(kernel.shape[1])
        ],
        axis=-1,
    )
    flat_windows = windows.reshape(rows_here * cols_here, -1)
    result = (
        jnp.dot(
            flat_windows, kernel.reshape(-1, kernel.shape[-1]), preferred_element_type=jnp.float32
        )
        + bias
    )
    return result.reshape(rows_here, cols_here, -1)


def on_device(
    encodings,
    spacing,
    ray_ids,
    live_count,
    pixel_of_ray,
    w_first,
    b_first,
    w_second,
    b_second,
    w_density,
    w_feature,
    kernel_one,
    bias_one,
    kernel_two,
    bias_two,
):
    encoded = encodings[0]
    spacing_all = spacing[0].T
    ray_index = ray_ids[0]
    live_total = live_count[0, 0]
    weights = (w_first[0], b_first[0], w_second[0], b_second[0], w_density[0], w_feature[0])
    ray_total = pixel_of_ray.shape[0]
    colour_zero = jnp.zeros((ray_total, FEAT), jnp.float32)
    depth_zero = jnp.zeros((ray_total,), jnp.float32)
    ray_colour, ray_depth = slot_terms(
        encoded, spacing_all, ray_index, live_total, weights, colour_zero, depth_zero
    )
    before = entering(
        ray_depth, "depth", lambda earlier, later: earlier + later, jnp.zeros_like(ray_depth)
    )
    partial_value = (jnp.exp(-before)[:, None] * ray_colour).astype(jnp.bfloat16)
    depth_count = lax.axis_size("depth")
    bundle_count = lax.axis_size("rays")
    image_wide = TW * depth_count
    pixel_row = pixel_of_ray // image_wide
    pixel_col = pixel_of_ray % image_wide
    tile_index = pixel_row // TH
    local_row = pixel_row % TH
    slot_of_ray = group_slots(tile_index, bundle_count)
    outgoing = (
        jnp.zeros((ray_total, FEAT), jnp.bfloat16)
        .at[slot_of_ray]
        .set(partial_value)
        .reshape(bundle_count, -1, FEAT)
    )
    targets = (
        jnp.zeros((ray_total,), jnp.int32)
        .at[slot_of_ray]
        .set(local_row * image_wide + pixel_col)
        .reshape(bundle_count, -1)
    )
    arrived, arrived_pix = (
        lax.all_to_all(outgoing, "rays", split_axis=0, concat_axis=0, tiled=True),
        lax.all_to_all(targets, "rays", split_axis=0, concat_axis=0, tiled=True),
    )
    tile_strip = (
        jnp.zeros((TH * image_wide, FEAT), jnp.bfloat16)
        .at[arrived_pix.reshape(-1)]
        .set(arrived.reshape(-1, FEAT))
    )
    tile_strip = tile_strip.reshape(TH, image_wide, FEAT)
    summed = lax.psum_scatter(
        tile_strip.astype(jnp.float32).astype(jnp.bfloat16),
        "depth",
        scatter_dimension=1,
        tiled=True,
    )
    hidden_image = jnp.maximum(convolve(summed, kernel_one, bias_one), 0.0).astype(jnp.bfloat16)
    return convolve(hidden_image, kernel_two, bias_two).astype(jnp.bfloat16)


def solution(mesh):
    in_specs = (
        P("depth", "rays", None, None),
        P("depth", None, "rays"),
        P("depth", "rays"),
        P("depth", "rays"),
        P("rays"),
        P("depth", None, None),
        P("depth", None),
        P("depth", None, None),
        P("depth", None),
        P("depth", None),
        P("depth", None, None),
        P(),
        P(),
        P(),
        P(),
    )
    out_specs = P("rays", "depth", None)
    return jax.shard_map(
        on_device, mesh=mesh, in_specs=in_specs, out_specs=out_specs, check_vma=False
    )
```

profile of v0, /device:TPU:15, one launch (start us, length us, event | category | flops | bytes accessed | tf_op | source)
XLA Modules:
  0.0 377.8 jit_solution(4696921252091570368)
XLA Ops:
  7.6 9.5 %reduce-window.6 = s32[32,64,128]{2,1,0:T(8,128)S(1)} reduce-window(s32[32,64,128]{2,1,0:T(8,128)S(1)} %fusion.26, s32[]{:T(128)} %constant.78.clone.1), window={size=1x1x128 pad=0_0x0_0x127_0}, to_apply=%region_0.1 | reduce-window | flops 33292288 | bytes 2097156 | tf_op jit(solution)/shard_map/reduce-window
  19.4 31.0 %scatter_custom_fusion = s32[8192]{0:T(1024)} fusion(s32[8192]{0:T(1024)S(1)} %compare_select_fusion.3, s32[8192]{0:T(1024)S(1)} %get-tuple-element.53, s32[]{:T(128)} %constant.78.clone.1), kind=kCustom, calls=%fused_computation.146 | custom fusion | bytes 32772 | tf_op jit(solution)/shard_map/scatter | solution.py:143
  50.4 11.0 %all-to-all-start = ((s32[32,1,256]{2,1,0:T(1,128)}), s32[32,1,256]{2,1,0:T(1,128)S(1)}, u32[]{:S(2)}, u32[]{:S(2)}) async-start(s32[32,1,256]{2,1,0:T(1,128)} %bitcast.3), calls=%async_computation | async-start | bytes 65536 | tf_op jit(solution)/shard_map/all_to_all | solution.py:148
  61.5 10.8 %fusion.3 = bf16[40960,128]{1,0:T(8,128)(2,1)} fusion(f32[128]{0:T(128)S(1)} %bitcast.106, bf16[1,5120,8,128]{3,2,1,0:T(8,128)(2,1)} %param.17, f32[128]{0:T(128)S(1)} %bitcast.107, bf16[1,128,128]{2,1,0:T(8,128)(2,1)S(1)} %copy-done.7, bf16[1,128,128]{2,1,0:T(8,128)(2,1)S(1)} %copy-done.8), kind=kOutput, calls=%fused_computation.11 | convolution fusion | flops 2715811840 | bytes 21038080 | tf_op jit(solution)/shard_map/dot_general | solution.py:43
  72.3 6.8 %fusion.53 = f32[1,40960]{1,0:T(1,128)S(1)} fusion(bf16[40960,128]{1,0:T(8,128)(2,1)} %fusion.3, bf16[1,128]{1,0:T(2,128)(2,1)S(1)} %copy-done.5), kind=kOutput, calls=%fused_computation.148 | convolution fusion | flops 10485760 | bytes 10649856 | tf_op jit(solution)/shard_map/dot_general | solution.py:46
  79.2 2.9 reshape.124
  82.2 2.2 copy.17
  84.4 3.3 fusion.56
  87.7 2.8 reduce_window_sum.28
  90.5 3.9 %subtract_multiply_fusion = f32[5120,8]{1,0:T(8,128)} fusion(f32[5120,8]{1,0:T(8,128)S(1)} %get-tuple-element.38, f32[5120,8]{1,0:T(8,128)} %reduce_window_sum.28), kind=kLoop, calls=%fused_computation.20 | loop fusion | flops 204800 | bytes 491520 | tf_op jit(solution)/shard_map/mul | solution.py:53
  95.2 27.2 %scatter_custom_fusion.1 = f32[8192]{0:T(1024)S(1)} fusion(s32[5120]{0:T(1024)S(1)} %bitcast.101, f32[5120]{0:T(1024)S(1)} %fusion.48, f32[]{:T(128)} %constant.89.clone.1), kind=kCustom, calls=%fused_computation.144 | custom fusion | flops 5120 | bytes 32772 | tf_op jit(solution)/shard_map/scatter-add | solution.py:57
  122.4 14.0 %all-gather = bf16[65536]{0:T(1024)(128)(2,1)S(1)} all-gather(bf16[8192]{0:T(1024)(128)(2,1)S(1)} %convert_element_type.47), channel_id=2, replica_groups=mesh['depth'=8,'rays'=32] {'depth'}, dimensions={0}, use_global_device_ids=true | all-gather | bytes 147456 | tf_op jit(solution)/shard_map/all_gather | solution.py:26
  137.0 13.9 %fusion.8 = f32[5120,1,128]{2,1,0:T(1,128)S(1)} fusion(f32[5120,8,1]{1,2,0:T(1,128)} %bitcast.94, bf16[40960,128]{1,0:T(8,128)(2,1)} %fusion.3, bf16[1,128,128]{2,1,0:T(8,128)(2,1)} %param.27), kind=kOutput, calls=%fused_computation.15 | convolution fusion | flops 1352663040 | bytes 13303808 | tf_op jit(solution)/shard_map/ns,nsf->nf/dot_general | solution.py:54
  151.0 32.4 %scatter_custom_fusion.2 = f32[8192,128]{1,0:T(8,128)} fusion(s32[5120]{0:T(1024)S(1)} %bitcast.102, f32[5120,128]{1,0:T(8,128)S(1)} %bitcast.93, f32[]{:T(128)} %constant.89.clone.1, f32[5120]{0:T(1024)S(1)} %fusion.47), kind=kCustom, calls=%fused_computation.18 | custom fusion | flops 1310720 | bytes 6836228 | tf_op jit(solution)/shard_map/scatter-add | solution.py:56
  183.4 26.8 %scatter_custom_fusion.3 = bf16[8192,128]{1,0:T(8,128)(2,1)} fusion(s32[8192]{0:T(1024)} %copy-done.3, f32[8192,128]{1,0:T(8,128)} %scatter_custom_fusion.2, f32[8192]{0:T(1024)S(1)} %negate_exponential_fusion, bf16[]{:T(256)} %constant.77.clone.1), kind=kCustom, calls=%fused_computation.21 | custom fusion | flops 2097152 | bytes 6324736 | tf_op jit(solution)/shard_map/scatter | solution.py:137
  210.2 9.2 %all-to-all-start.1 = ((bf16[32,256,128]{2,1,0:T(8,128)(2,1)}), bf16[32,256,128]{2,1,0:T(8,128)(2,1)S(1)}, u32[]{:S(2)}, u32[]{:S(2)}) async-start(bf16[32,256,128]{2,1,0:T(8,128)(2,1)} %bitcast.26), calls=%async_computation.1 | async-start | bytes 4194304 | tf_op jit(solution)/shard_map/all_to_all | solution.py:147
  219.5 49.9 %all-to-all-done.1 = bf16[32,256,128]{2,1,0:T(8,128)(2,1)S(1)} async-done(((bf16[32,256,128]{2,1,0:T(8,128)(2,1)}), bf16[32,256,128]{2,1,0:T(8,128)(2,1)S(1)}, u32[]{:S(2)}, u32[]{:S(2)}) %all-to-all-start.1) | async-done | bytes 2097184 | tf_op jit(solution)/shard_map/all_to_all | solution.py:147
  269.4 22.6 %scatter_custom_fusion.4 = bf16[8192,128]{1,0:T(8,128)(2,1)} fusion(s32[8192]{0:T(1024)S(1)} %bitcast.100, bf16[8192,128]{1,0:T(8,128)(2,1)S(1)} %bitcast.95, bf16[]{:T(256)} %constant.77.clone.1), kind=kCustom, calls=%fused_computation.36 | custom fusion | bytes 2097154 | tf_op jit(solution)/shard_map/scatter | solution.py:153
  292.0 30.8 %reduce-scatter.2.cloned.1.call-done = bf16[16,64,128]{2,1,0:T(8,128)(2,1)} async-done(((bf16[16,512,128]{2,1,0:T(8,128)(2,1)}), bf16[16,64,128]{2,1,0:T(8,128)(2,1)}) %reduce-scatter.2.cloned.1.call-update) | async-done | bytes 262160 | tf_op jit(solution)/shard_map/reduce_scatter | solution.py:156
  323.7 2.4 collective-permute-start
  326.0 2.6 collective-permute-start.1
  328.6 2.4 collective-permute-done.1
  331.8 3.2 collective-permute-start.2
  335.0 2.1 collective-permute-start.3
  337.1 4.7 %collective-permute-done.3 = bf16[2,68,128]{2,1,0:T(8,128)(2,1)S(1)} collective-permute-done((bf16[2,68,128]{2,1,0:T(8,128)(2,1)S(1)}, bf16[2,68,128]{2,1,0:T(8,128)(2,1)S(1)}, u32[]{:S(2)}, u32[]{:S(2)}) %collective-permute-start.3) | collective-permute-done | bytes 34848 | tf_op jit(solution)/shard_map/ppermute | solution.py:19
  347.8 3.9 %collective-permute-start.4 = (bf16[16,2,128]{2,1,0:T(2,128)(2,1)S(1)}, bf16[16,2,128]{2,1,0:T(2,128)(2,1)S(1)}, u32[]{:S(2)}, u32[]{:S(2)}) collective-permute-start(bf16[16,2,128]{2,1,0:T(2,128)(2,1)S(1)} %get-tuple-element.47), channel_id=1, source_target_pairs={{0,32},{32,64},{64,96},{96,128},{128,160},{160,192},{192,224},{1,3... | collective-permute-start | bytes 24584 | tf_op jit(solution)/shard_map/ppermute | solution.py:18
  351.8 2.0 collective-permute-start.5
  353.8 3.0 collective-permute-done.5
  356.8 1.9 collective-permute-start.6
  358.7 3.4 collective-permute-start.7
  362.1 3.4 collective-permute-done.7
  368.4 2.6 fusion.20
  (114 shorter events, 14.3 us)
Async XLA Ops:
  6.5 339.4 %copy-start = (bf16[5,5,128,128]{3,2,1,0:T(8,128)(2,1)S(1)}, bf16[5,5,128,128]{3,2,1,0:T(8,128)(2,1)}, u32[]{:S(2)}) copy-start(bf16[5,5,128,128]{3,2,1,0:T(8,128)(2,1)} %param.28) | copy-start | bytes 2457604
  6.5 54.9 %copy-start.10 = (f32[1,128]{1,0:T(1,128)S(1)}, f32[1,128]{1,0:T(1,128)}, u32[]{:S(2)}) copy-start(f32[1,128]{1,0:T(1,128)} %param.23) | copy-start | bytes 1540
  6.5 54.9 %copy-start.9 = (f32[1,128]{1,0:T(1,128)S(1)}, f32[1,128]{1,0:T(1,128)}, u32[]{:S(2)}) copy-start(f32[1,128]{1,0:T(1,128)} %param.25) | copy-start | bytes 1540
  6.5 54.9 %copy-start.8 = (bf16[1,128,128]{2,1,0:T(8,128)(2,1)S(1)}, bf16[1,128,128]{2,1,0:T(8,128)(2,1)}, u32[]{:S(2)}) copy-start(bf16[1,128,128]{2,1,0:T(8,128)(2,1)} %param.22) | copy-start | bytes 98308
  6.5 54.9 %copy-start.7 = (bf16[1,128,128]{2,1,0:T(8,128)(2,1)S(1)}, bf16[1,128,128]{2,1,0:T(8,128)(2,1)}, u32[]{:S(2)}) copy-start(bf16[1,128,128]{2,1,0:T(8,128)(2,1)} %param.24) | copy-start | bytes 98308
  19.4 52.9 %copy-start.3 = (s32[8192]{0:T(1024)}, s32[8192]{0:T(1024)S(1)}, u32[]{:S(2)}) copy-start(s32[8192]{0:T(1024)S(1)} %compare_select_fusion.3) | copy-start | bytes 98308
  50.4 159.8 %all-to-all-start = ((s32[32,1,256]{2,1,0:T(1,128)}), s32[32,1,256]{2,1,0:T(1,128)S(1)}, u32[]{:S(2)}, u32[]{:S(2)}) async-start(s32[32,1,256]{2,1,0:T(1,128)} %bitcast.3), calls=%async_computation | async-start | bytes 65536 | tf_op jit(solution)/shard_map/all_to_all | solution.py:148
  61.5 10.8 %copy-start.5 = (bf16[1,128]{1,0:T(2,128)(2,1)S(1)}, bf16[1,128]{1,0:T(2,128)(2,1)}, u32[]{:S(2)}) copy-start(bf16[1,128]{1,0:T(2,128)(2,1)} %param.26) | copy-start | bytes 772
  72.3 9.9 %copy-start.2 = (f32[1,8,5120]{2,1,0:T(8,128)S(1)}, f32[1,8,5120]{2,1,0:T(8,128)}, u32[]{:S(2)}) copy-start(f32[1,8,5120]{2,1,0:T(8,128)} %param.18) | copy-start | bytes 491524
  87.7 7.4 %copy-start.4 = (s32[1,5120]{1,0:T(1,128)S(1)}, s32[1,5120]{1,0:T(1,128)}, u32[]{:S(2)}) copy-start(s32[1,5120]{1,0:T(1,128)} %param.19) | copy-start | bytes 61444
  210.2 59.2 %all-to-all-start.1 = ((bf16[32,256,128]{2,1,0:T(8,128)(2,1)}), bf16[32,256,128]{2,1,0:T(8,128)(2,1)S(1)}, u32[]{:S(2)}, u32[]{:S(2)}) async-start(bf16[32,256,128]{2,1,0:T(8,128)(2,1)} %bitcast.26), calls=%async_computation.1 | async-start | bytes 4194304 | tf_op jit(solution)/shard_map/all_to_all | solution.py:147
  219.4 103.4 %reduce-scatter.2.cloned.1.call-start = ((), (), s32[]{:S(2)}) async-start(), calls=%async_computation.3 | async-start | bytes 2359296 | tf_op jit(solution)/shard_map/reduce_scatter | solution.py:156
  322.8 21.4 %copy-start.1 = (bf16[16,64,128]{2,1,0:T(8,128)(2,1)S(1)}, bf16[16,64,128]{2,1,0:T(8,128)(2,1)}, u32[]{:S(2)}) copy-start(bf16[16,64,128]{2,1,0:T(8,128)(2,1)} %reduce-scatter.2.cloned.1.call-done) | copy-start | bytes 786436
  323.7 5.0 %collective-permute-start = (bf16[16,2,128]{2,1,0:T(2,128)(2,1)S(1)}, bf16[16,2,128]{2,1,0:T(2,128)(2,1)S(1)}, u32[]{:S(2)}, u32[]{:S(2)}) collective-permute-start(bf16[16,2,128]{2,1,0:T(2,128)(2,1)S(1)} %get-tuple-element.51), channel_id=1, source_target_pairs={{0,32},{32,64},{64,96},{96,128},{128,160},{160,192},{192,224},{1,3... | collective-permute-start | bytes 24584 | tf_op jit(solution)/shard_map/ppermute | solution.py:18
  326.0 5.0 %collective-permute-start.1 = (bf16[16,2,128]{2,1,0:T(2,128)(2,1)S(1)}, bf16[16,2,128]{2,1,0:T(2,128)(2,1)S(1)}, u32[]{:S(2)}, u32[]{:S(2)}) collective-permute-start(bf16[16,2,128]{2,1,0:T(2,128)(2,1)S(1)} %get-tuple-element.52), channel_id=1, source_target_pairs={{32,0},{64,32},{96,64},{128,96},{160,128},{192,160},{224,192},{33,... | collective-permute-start | bytes 24584 | tf_op jit(solution)/shard_map/ppermute | solution.py:19
  331.8 5.3 %collective-permute-start.2 = (bf16[2,68,128]{2,1,0:T(8,128)(2,1)S(1)}, bf16[2,68,128]{2,1,0:T(8,128)(2,1)S(1)}, u32[]{:S(2)}, u32[]{:S(2)}) collective-permute-start(bf16[2,68,128]{2,1,0:T(8,128)(2,1)S(1)} %get-tuple-element.46), channel_id=1, source_target_pairs={{0,1},{1,2},{2,3},{3,4},{4,5},{5,6},{6,7},{7,8},{8,9},{9,10},{10,1... | collective-permute-start | bytes 104456 | tf_op jit(solution)/shard_map/ppermute | solution.py:18
  335.0 6.8 %collective-permute-start.3 = (bf16[2,68,128]{2,1,0:T(8,128)(2,1)S(1)}, bf16[2,68,128]{2,1,0:T(8,128)(2,1)S(1)}, u32[]{:S(2)}, u32[]{:S(2)}) collective-permute-start(bf16[2,68,128]{2,1,0:T(8,128)(2,1)S(1)} %get-tuple-element.45), channel_id=1, source_target_pairs={{1,0},{2,1},{3,2},{4,3},{5,4},{6,5},{7,6},{8,7},{9,8},{10,9},{11,1... | collective-permute-start | bytes 104456 | tf_op jit(solution)/shard_map/ppermute | solution.py:19
  343.2 2.7 copy-start.11
  347.8 5.9 %collective-permute-start.4 = (bf16[16,2,128]{2,1,0:T(2,128)(2,1)S(1)}, bf16[16,2,128]{2,1,0:T(2,128)(2,1)S(1)}, u32[]{:S(2)}, u32[]{:S(2)}) collective-permute-start(bf16[16,2,128]{2,1,0:T(2,128)(2,1)S(1)} %get-tuple-element.47), channel_id=1, source_target_pairs={{0,32},{32,64},{64,96},{96,128},{128,160},{160,192},{192,224},{1,3... | collective-permute-start | bytes 24584 | tf_op jit(solution)/shard_map/ppermute | solution.py:18
  351.8 5.0 %collective-permute-start.5 = (bf16[16,2,128]{2,1,0:T(2,128)(2,1)S(1)}, bf16[16,2,128]{2,1,0:T(2,128)(2,1)S(1)}, u32[]{:S(2)}, u32[]{:S(2)}) collective-permute-start(bf16[16,2,128]{2,1,0:T(2,128)(2,1)S(1)} %get-tuple-element.48), channel_id=1, source_target_pairs={{32,0},{64,32},{96,64},{128,96},{160,128},{192,160},{224,192},{33,... | collective-permute-start | bytes 24584 | tf_op jit(solution)/shard_map/ppermute | solution.py:19
  356.8 5.3 %collective-permute-start.6 = (bf16[2,68,128]{2,1,0:T(8,128)(2,1)S(1)}, bf16[2,68,128]{2,1,0:T(8,128)(2,1)S(1)}, u32[]{:S(2)}, u32[]{:S(2)}) collective-permute-start(bf16[2,68,128]{2,1,0:T(8,128)(2,1)S(1)} %get-tuple-element.42), channel_id=1, source_target_pairs={{0,1},{1,2},{2,3},{3,4},{4,5},{5,6},{6,7},{7,8},{8,9},{9,10},{10,1... | collective-permute-start | bytes 104456 | tf_op jit(solution)/shard_map/ppermute | solution.py:18
  358.7 6.8 %collective-permute-start.7 = (bf16[2,68,128]{2,1,0:T(8,128)(2,1)S(1)}, bf16[2,68,128]{2,1,0:T(8,128)(2,1)S(1)}, u32[]{:S(2)}, u32[]{:S(2)}) collective-permute-start(bf16[2,68,128]{2,1,0:T(8,128)(2,1)S(1)} %get-tuple-element.41), channel_id=1, source_target_pairs={{1,0},{2,1},{3,2},{4,3},{5,4},{6,5},{7,6},{8,7},{9,8},{10,9},{11,1... | collective-permute-start | bytes 104456 | tf_op jit(solution)/shard_map/ppermute | solution.py:19
  365.6 2.7 copy-start.6
  365.6 2.7 copy-start.12
Sparse Core Ops, SparseCore 0:
  292.2 30.6 reduce-scatter.1
where the time goes:
time: 382 us; the launch traced here: 378 us
  other arithmetic  112 us (29%)
  waiting for transfers between devices  94.2 us (25%)
  local copies, waits for them, and re-layouts  65.1 us (17%)
  starting transfers between devices  41.7 us (11%)
  matrix products  36 us (9%)
  between operations  14.8 us (4%)
  blocking collectives  14 us (4%)
    all_to_all x1, waiting for transfers between devices, on_device(): lax.all_to_all(outgoing, 'rays', split_axis=0, concat_axis=0, tiled=True)  49.9 us
    scatter-add x1, other arithmetic, slot_terms(): colour_out = colour_base.at[ray_index].add(colour * live_mask[:, None])  32.4 us
    scatter x1, local copies, waits for them, and re-layouts, on_device(): targets = jnp.zeros((ray_total,), jnp.int32).at[slot_of_ray].set(local_ro...  31 us
    reduce_scatter x1, waiting for transfers between devices, on_device(): lax.psum_scatter(tile_strip.astype(jnp.float32).astype(jnp.bfloat16), 'de...  30.8 us
    scatter-add x1, other arithmetic, slot_terms(): depth_base.at[ray_index].add(jnp.sum(opacity, axis=1) * live_mask)  27.2 us
    scatter x1, other arithmetic, on_device(): outgoing = jnp.zeros((ray_total, FEAT), jnp.bfloat16).at[slot_of_ray].set...  26.8 us
    scatter x1, local copies, waits for them, and re-layouts, on_device(): tile_strip = jnp.zeros((TH * image_wide, FEAT), jnp.bfloat16).at[arrived_...  22.6 us
    all_gather x1, blocking collectives, entering(): gathered = lax.all_gather(array.astype(jnp.bfloat16), axis)  14 us
  transfers between devices with their start and end apart: 11, of which 6 were waited for; matrix products, arithmetic and copies ran while one was open for 35% of the time, Pallas kernels for 0%

commit v1 on v0

v1 whole, which is shorter than its diff:
```python
import functools

import jax
import jax.numpy as jnp
from jax import lax
from jax.experimental import pallas as pl
from jax.experimental.pallas import tpu as pltpu
from jax.sharding import PartitionSpec as P

FEAT = 128
SAMPLES = 8
TH = 16
TW = 64
WIDE = 512
HEIGHT = 512
SLOTS = 5120
RAYS = 8192
LANES = 128
BLOCKS = 256
HALO = 4
PITCH = TW + 16
PIECE = 1024
PACK = PIECE + 16
SUPER = 256
f32 = jnp.float32
bf16 = jnp.bfloat16
i32 = jnp.int32


def dot_nt(lhs, rhs):
    return lax.dot_general(lhs, rhs, (((1,), (1,)), ((), ())), preferred_element_type=f32)


def dot_nn(lhs, rhs):
    return jnp.dot(lhs, rhs, preferred_element_type=f32)


def iota(shape, axis):
    return lax.broadcasted_iota(i32, shape, axis)


def as_bf16(mask):
    return jnp.where(mask, 1.0, 0.0).astype(bf16)


def index_kernel(where_ref, pixel_ref, ids_ref, pos_ref, info_ref, hi_scr, lo_scr):
    my_core, my_y, bundle = where_ref[0], where_ref[1], where_ref[2]
    pixel = pixel_ref[...]
    row, col = pixel >> 9, pixel & (WIDE - 1)
    block_col = col >> 6
    core_rel = (block_col & 1) ^ my_core
    y_rel = ((block_col >> 1) - my_y) & 3
    group = core_rel * 128 + y_rel * 32 + (row >> 4)
    local_row, local_col = (row & (TH - 1)).astype(f32), (col & (TW - 1)).astype(f32)
    upper = as_bf16(iota((LANES, 2 * LANES), 0) < iota((LANES, 2 * LANES), 1))
    group_iota = iota((BLOCKS, LANES), 0)
    carry = jnp.zeros((BLOCKS, LANES), f32)
    own = jnp.zeros((8, 2 * LANES), f32)
    lane_iota = iota((LANES, LANES), 0)
    for j in range(RAYS // LANES):
        g = group[j : j + 1, :]
        hit = group_iota == g
        member = jnp.where(hit, 1.0, 0.0)
        counts = dot_nn(member.astype(bf16), upper)
        rank = jnp.sum(member * (counts[:, :LANES] + carry), axis=0, keepdims=True)
        carry = carry + counts[:, LANES:]
        hi = g >> 2
        lo = (g & 3) * 32 + rank.astype(i32)
        hi_scr[j : j + 1, :] = hi.astype(f32)
        lo_scr[j : j + 1, :] = lo.astype(f32)
        mine = as_bf16(iota((8, LANES), 0) == hi)
        at = lane_iota == lo
        wanted = jnp.concatenate(
            [
                jnp.where(at, local_row[j : j + 1, :], 0.0).astype(bf16),
                jnp.where(at, local_col[j : j + 1, :], 0.0).astype(bf16),
            ],
            axis=0,
        )
        own = own + dot_nt(mine, wanted)
    own_row, own_col = own[:, :LANES], own[:, LANES:]
    lane8 = iota((8, LANES), 1)
    quarter = bundle & 3
    for q in range(4):
        shift = ((quarter - q) & 3) * 32
        keep = (lane8 >> 5) == quarter
        info_ref[q, 0] = jnp.where(keep, pltpu.roll(own_row, shift, 1), 0.0)
        info_ref[q, 1] = jnp.where(keep, pltpu.roll(own_col, shift, 1), 0.0)
    table = jnp.concatenate([hi_scr[...], lo_scr[...]], axis=1).astype(bf16)
    high_iota = iota((RAYS // LANES, LANES), 0)
    for j in range(SLOTS // LANES):
        ids = ids_ref[j : j + 1, :]
        high = as_bf16(high_iota == (ids >> 7))
        found = lax.dot_general(table, high, (((0,), (0,)), ((), ())), preferred_element_type=f32)
        low = lane_iota == (ids & (LANES - 1))
        hi = jnp.sum(jnp.where(low, found[:LANES], 0.0), axis=0, keepdims=True)
        lo = jnp.sum(jnp.where(low, found[LANES:], 0.0), axis=0, keepdims=True)
        pos_ref[j : j + 1, :] = hi.astype(i32) * LANES + lo.astype(i32)


def segment_kernel(
    pos_smem,
    live_smem,
    enc_ref,
    gap_ref,
    pos_ref,
    w1_ref,
    b1_ref,
    w2_ref,
    b2_ref,
    wd_ref,
    wf_ref,
    near_ref,
    far_ref,
    spread,
    colour,
    depth,
):
    step = pl.program_id(0)
    per_step = enc_ref.shape[0] // (SUPER * SAMPLES)
    live = live_smem[0]

    @pl.when(step == 0)
    def _():
        spread[...] = jnp.zeros_like(spread)

    lane = iota((8, SUPER), 1)
    row8 = iota((8, SUPER), 0)
    sample = lane & 7
    of_slot = iota((32, SUPER), 0) == (iota((32, SUPER), 1) >> 3)
    pick = jnp.concatenate(
        [
            as_bf16(
                iota((SUPER, LANES), 0) == (iota((SUPER, LANES), 1) - 32 * q) * 8 + 7
            )
            for q in range(4)
        ],
        axis=1,
    )
    half = SUPER * SAMPLES // 2
    for part in range(per_step):
        base = part * SUPER * SAMPLES
        x = jnp.concatenate(
            [enc_ref[base : base + half, :], enc_ref[base + half : base + 2 * half, :]], axis=1
        )
        h1 = jnp.maximum(dot_nn(x, w1_ref[...]) + b1_ref[...], 0.0).astype(bf16)
        h2 = jnp.maximum(dot_nn(h1, w2_ref[...]) + b2_ref[...], 0.0).astype(bf16)
        pre = jnp.zeros((8, SUPER), f32)
        for i in range(4):
            pre = pre + dot_nt(wd_ref[i], h2[i * SUPER : (i + 1) * SUPER, :])
        soft = jnp.maximum(pre, 0.0) + jnp.log1p(jnp.exp(-jnp.abs(pre)))
        opacity = soft * gap_ref[part * 8 : part * 8 + 8, :]
        inc = opacity
        for shift in (1, 2, 4):
            inc = inc + jnp.where(sample >= shift, pltpu.roll(inc, shift, 1), 0.0)
        weight = jnp.exp(opacity - inc) * (1.0 - jnp.exp(-opacity))
        slot = (step * per_step + part) * SUPER + row8 * 32 + (lane >> 3)
        alive = slot < live
        weight = jnp.where(alive, weight, 0.0)
        inc = jnp.where(alive, inc, 0.0)
        inc_hi = inc.astype(bf16)
        inc_lo = (inc - inc_hi.astype(f32)).astype(bf16)
        picked = dot_nn(inc_hi, pick) + dot_nn(inc_lo, pick)
        lined = jnp.zeros((8, LANES), f32)
        r8 = iota((8, LANES), 0)
        for q in range(4):
            lined = lined + jnp.where((r8 & 3) == q, picked[:, q * LANES : (q + 1) * LANES], 0.0)
        block = (step * per_step + part) * 2
        depth[pl.ds(block, 1), :] = jnp.sum(lined[:4], axis=0, keepdims=True)
        depth[pl.ds(block + 1, 1), :] = jnp.sum(lined[4:], axis=0, keepdims=True)
        gathered = [None] * 8
        for i in range(4):
            left = jnp.where(of_slot, weight[i : i + 1, :], 0.0)
            right = jnp.where(of_slot, weight[i + 4 : i + 5, :], 0.0)
            both = jnp.concatenate([left, right], axis=0).astype(bf16)
            summed = dot_nn(both, h2[i * SUPER : (i + 1) * SUPER, :])
            gathered[i] = summed[:32, :LANES]
            gathered[i + 4] = summed[32:, LANES:]
        mixed = jnp.concatenate(gathered, axis=0).astype(bf16)
        colour[...] = dot_nn(mixed, wf_ref[...])
        first = (step * per_step + part) * SUPER
        for s in range(SUPER):
            spread[pl.ds(pos_smem[first + s], 1), :] = colour[s : s + 1, :]

    @pl.when(step == pl.num_programs(0) - 1)
    def _():
        table = jnp.zeros((RAYS // LANES, 2 * LANES), f32)
        for j in range(SLOTS // LANES):
            at = pos_ref[j : j + 1, :]
            here = depth[j : j + 1, :]
            high = as_bf16(iota((RAYS // LANES, LANES), 0) == (at >> 7))
            low = iota((LANES, LANES), 0) == (at & (LANES - 1))
            coarse = here.astype(bf16).astype(f32)
            wanted = jnp.concatenate(
                [
                    jnp.where(low, coarse, 0.0).astype(bf16),
                    jnp.where(low, here - coarse, 0.0).astype(bf16),
                ],
                axis=0,
            )
            table = table + dot_nt(high, wanted)
        for g in range(4):
            for k, out in enumerate((near_ref, far_ref)):
                at = (4 * k + g) * PIECE
                out[g, :PIECE, :] = spread[at : at + PIECE, :].astype(bf16)
                rows = slice((4 * k + g) * 8, (4 * k + g) * 8 + 8)
                out[g, PIECE:, :] = jnp.concatenate(
                    [table[rows, :LANES], table[rows, LANES:]], axis=0
                ).astype(bf16)


def read_depth(ref):
    rows = ref[PIECE:, :].astype(f32)
    return rows[:8] + rows[8:]


def scaled(ref, factors, i):
    return ref[i * LANES : (i + 1) * LANES, :].astype(f32) * factors[:, i : i + 1]


def pair_kernel(where_ref, near_ref, arrived_ref, *outs):
    first = where_ref[0] == 0
    for g in range(4):
        mine, other = near_ref.at[g], arrived_ref.at[g]
        d_mine, d_other = read_depth(mine), read_depth(other)
        fade = jnp.exp(-jnp.where(first, d_mine, d_other))
        one = jnp.ones_like(fade)
        f_mine = jnp.where(first, one, fade).T
        f_other = jnp.where(first, fade, one).T
        for i in range(8):
            outs[g][i * LANES : (i + 1) * LANES, :] = (
                scaled(mine, f_mine, i) + scaled(other, f_other, i)
            ).astype(bf16)
        both = d_mine + d_other
        coarse = both.astype(bf16).astype(f32)
        outs[g][PIECE:, :] = jnp.concatenate([coarse, both - coarse], axis=0).astype(bf16)


def merge_kernel(where_ref, p0_ref, p1_ref, p2_ref, p3_ref, info_ref, out_ref):
    y = where_ref[1]
    pieces = (p0_ref, p1_ref, p2_ref, p3_ref)
    places = [(y - k) & 3 for k in range(4)]
    depths = [read_depth(ref) for ref in pieces]
    factors = []
    for a in range(4):
        before = jnp.zeros_like(depths[0])
        for b in range(4):
            if b != a:
                before = before + jnp.where(places[b] < places[a], depths[b], 0.0)
        factors.append(jnp.exp(-before).T)
    for i in range(8):
        total = scaled(pieces[0], factors[0], i)
        for k in range(1, 4):
            total = total + scaled(pieces[k], factors[k], i)
        total = total.astype(bf16)
        for q in range(4):
            tile = i * 4 + q
            out_ref[tile, :32, :] = total[q * 32 : q * 32 + 32, :]
            extra = jnp.concatenate(
                [
                    info_ref[q, 0, i : i + 1, :],
                    info_ref[q, 1, i : i + 1, :],
                    jnp.zeros((6, LANES), f32),
                ],
                axis=0,
            )
            out_ref[tile, 32:, :] = extra.astype(bf16)


def place_kernel(in_ref, out_ref):
    total = jnp.zeros((TH * TW, FEAT), f32)
    pixel_iota = iota((TH * TW, LANES), 0)
    for g in range(8):
        rows = jnp.concatenate([in_ref[4 * g + q, :32, :] for q in range(4)], axis=0)
        place = in_ref[4 * g, 32:, :].astype(f32)
        for q in range(1, 4):
            place = place + in_ref[4 * g + q, 32:, :].astype(f32)
        pixel = (place[0:1, :] * TW + place[1:2, :]).astype(i32)
        total = total + dot_nn(as_bf16(pixel_iota == pixel), rows)
    out_ref[...] = total.astype(bf16)


def whole(shape):
    return pl.BlockSpec(shape, lambda *_: (0,) * len(shape))


def shape_of(shape, dtype):
    return jax.ShapeDtypeStruct(shape, dtype)


VMEM = pl.BlockSpec(memory_space=pltpu.VMEM)
SMEM = pl.BlockSpec(memory_space=pltpu.SMEM)


def segments(pos, live, enc, gaps, w1, b1, w2, b2, wd, wf, per_step=2):
    def twice(w):
        zero = jnp.zeros_like(w)
        return jnp.concatenate(
            [jnp.concatenate([w, zero], axis=1), jnp.concatenate([zero, w], axis=1)], axis=0
        )

    eye = jnp.eye(8, dtype=bf16)
    heads = jnp.stack(
        [
            jnp.concatenate([eye[i][:, None] * wd[None], eye[i + 4][:, None] * wd[None]], axis=1)
            for i in range(4)
        ]
    )
    rows = per_step * SUPER * SAMPLES
    steps = SLOTS * SAMPLES // rows
    out = shape_of((4, PACK, FEAT), bf16)
    return pl.pallas_call(
        segment_kernel,
        grid_spec=pltpu.PrefetchScalarGridSpec(
            num_scalar_prefetch=2,
            grid=(steps,),
            in_specs=[
                pl.BlockSpec((rows, FEAT), lambda i, *_: (i, 0)),
                pl.BlockSpec((per_step * 8, SUPER), lambda i, *_: (i, 0)),
                whole((SLOTS // LANES, LANES)),
                whole((256, 256)),
                whole((1, 256)),
                whole((256, 256)),
                whole((1, 256)),
                whole((4, 8, 256)),
                whole((128, 128)),
            ],
            out_specs=[whole((4, PACK, FEAT))] * 2,
            scratch_shapes=[
                pltpu.VMEM((RAYS, FEAT), f32),
                pltpu.VMEM((SUPER, FEAT), f32),
                pltpu.VMEM((SLOTS // LANES, LANES), f32),
            ],
        ),
        out_shape=[out, out],
        name="segments",
    )(
        pos.reshape(SLOTS),
        live,
        enc,
        gaps,
        pos,
        twice(w1),
        jnp.tile(b1, 2)[None],
        twice(w2),
        jnp.tile(b2, 2)[None],
        heads,
        wf,
    )


def exchanged(low, high, axis):
    size = lax.axis_size(axis)
    up = [(i, i + 1) for i in range(size - 1)]
    down = [(j, i) for i, j in up]
    return lax.ppermute(high, axis, up), lax.ppermute(low, axis, down)


def shift_columns(source, shifted, rows, first):
    for j in range(5):
        shifted[:rows, j * LANES : (j + 1) * LANES] = source[first + j : first + j + rows, :].astype(
            bf16
        )


def conv_kernel(
    where_ref, mid_ref, top_ref, low_ref, k1_ref, b1_ref, k2_ref, b2_ref, out_ref, rows, shifted
):
    place, tile = where_ref[1] * 2 + where_ref[0], where_ref[2]
    rows[: 4 * PITCH, :] = top_ref[...].astype(f32)
    rows[4 * PITCH : 20 * PITCH, :] = mid_ref[...].astype(f32)
    rows[20 * PITCH : 24 * PITCH, :] = low_ref[...].astype(f32)
    rows[24 * PITCH :, :] = jnp.zeros((16, FEAT), f32)
    shift_columns(rows, shifted, 24 * PITCH, 4)
    flat = iota((4 * PITCH, FEAT), 0)
    y_in, x = flat // PITCH, flat % PITCH
    col = place * TW - 2 + x
    for part in range(5):
        base = part * 4 * PITCH
        total = jnp.zeros((4 * PITCH, FEAT), f32) + b1_ref[...]
        for i in range(5):
            at = base + i * PITCH
            total = total + dot_nn(shifted[at : at + 4 * PITCH, :], k1_ref[i])
        row = tile * TH - 2 + part * 4 + y_in
        inside = (row >= 0) & (row < HEIGHT) & (col >= 0) & (col < WIDE)
        rows[base : base + 4 * PITCH, :] = jnp.where(inside, jnp.maximum(total, 0.0), 0.0)
    shift_columns(rows, shifted, 20 * PITCH, 0)
    for part in range(4):
        base = part * 4 * PITCH
        total = jnp.zeros((4 * PITCH, FEAT), f32) + b2_ref[...]
        for i in range(5):
            at = base + i * PITCH
            total = total + dot_nn(shifted[at : at + 4 * PITCH, :], k2_ref[i])
        total = total.astype(bf16)
        for y in range(4):
            out_ref[part * 4 + y] = total[y * PITCH : y * PITCH + TW, :]


def index_call(where, pixel, ids):
    return pl.pallas_call(
        index_kernel,
        in_specs=[SMEM, VMEM, VMEM],
        out_specs=[VMEM, VMEM],
        out_shape=[shape_of((SLOTS // LANES, LANES), i32), shape_of((4, 2, 8, LANES), f32)],
        scratch_shapes=[pltpu.VMEM((RAYS // LANES, LANES), f32)] * 2,
        name="index",
    )(where, pixel.reshape(RAYS // LANES, LANES), ids.reshape(SLOTS // LANES, LANES))


def on_device(
    encodings,
    spacing,
    ray_ids,
    live_count,
    pixel_of_ray,
    w_first,
    b_first,
    w_second,
    b_second,
    w_density,
    w_feature,
    kernel_one,
    bias_one,
    kernel_two,
    bias_two,
):
    place = lax.axis_index("depth")
    tile = lax.axis_index("rays")
    where = jnp.stack([place & 1, place >> 1, tile]).astype(i32)
    pos, info = index_call(where, pixel_of_ray, ray_ids)
    gaps = spacing[0].T.reshape(SLOTS // 32, SUPER)
    near, far = segments(
        pos,
        live_count.reshape(1),
        encodings.reshape(SLOTS * SAMPLES, FEAT),
        gaps,
        w_first[0],
        b_first[0],
        w_second[0],
        b_second[0],
        w_density[0],
        w_feature[0],
    )
    arrived = lax.ppermute(far, "depth", [(i, i ^ 1) for i in range(8)])
    piece = shape_of((PACK, FEAT), bf16)
    pieces = pl.pallas_call(
        pair_kernel,
        in_specs=[SMEM, VMEM, VMEM],
        out_specs=[VMEM] * 4,
        out_shape=[piece] * 4,
        name="pair",
    )(where, near, arrived)
    got = [
        lax.ppermute(pieces[k], "depth", [(i, (i + 2 * k) % 8) for i in range(8)])
        for k in range(1, 4)
    ]
    outgoing = pl.pallas_call(
        merge_kernel,
        in_specs=[SMEM] + [VMEM] * 5,
        out_specs=VMEM,
        out_shape=shape_of((32, 40, FEAT), bf16),
        name="merge",
    )(where, pieces[0], *got, info)
    incoming = lax.all_to_all(outgoing, "rays", split_axis=0, concat_axis=0, tiled=True)
    image = pl.pallas_call(
        place_kernel,
        in_specs=[VMEM],
        out_specs=VMEM,
        out_shape=shape_of((TH * TW, FEAT), bf16),
        name="place",
    )(incoming)
    block = image.reshape(TH, TW, FEAT)
    before, after = exchanged(block[:, :8], block[:, TW - 8 :], "depth")
    middle = jnp.concatenate([before, block, after], axis=1)
    top, low = exchanged(middle[:HALO], middle[TH - HALO :], "rays")
    return pl.pallas_call(
        conv_kernel,
        in_specs=[SMEM] + [VMEM] * 7,
        out_specs=VMEM,
        out_shape=shape_of((TH, TW, FEAT), bf16),
        scratch_shapes=[
            pltpu.VMEM((24 * PITCH + 16, FEAT), f32),
            pltpu.VMEM((24 * PITCH, 5 * FEAT), bf16),
        ],
        name="conv",
    )(
        where,
        middle.reshape(TH * PITCH, FEAT),
        top.reshape(HALO * PITCH, FEAT),
        low.reshape(HALO * PITCH, FEAT),
        kernel_one.reshape(5, 5 * FEAT, FEAT),
        bias_one[None],
        kernel_two.reshape(5, 5 * FEAT, FEAT),
        bias_two[None],
    )


def solution(mesh):
    in_specs = (
        P("depth", "rays", None, None),
        P("depth", None, "rays"),
        P("depth", "rays"),
        P("depth", "rays"),
        P("rays"),
        P("depth", None, None),
        P("depth", None),
        P("depth", None, None),
        P("depth", None),
        P("depth", None),
        P("depth", None, None),
        P(),
        P(),
        P(),
        P(),
    )
    return jax.shard_map(
        on_device, mesh=mesh, in_specs=in_specs, out_specs=P("rays", "depth", None), check_vma=False
    )
```

time: 382 us -> 136 us (0.36)
  the two profiles are of different devices: /device:TPU:15 before, /device:TPU:41 now
where the time goes in v1:
time: 136 us
  Pallas kernels  60 us (44%)
  waiting for transfers between devices  23.6 us (17%)
  blocking collectives  21.7 us (16%)
  starting transfers between devices  18.5 us (14%)
  local copies, waits for them, and re-layouts  8.15 us (6%)
  other arithmetic  2.96 us (2%)
    pallas_call x1, Pallas kernels, segments(): pl.pallas_call(segment_kernel, grid_spec=pltpu.PrefetchScalarGridSpec(num...  34.8 us
    all_to_all x1, blocking collectives, on_device(): lax.all_to_all(outgoing, 'rays', split_axis=0, concat_axis=0, tiled=True)  21.7 us
    ppermute x4, starting transfers between devices, exchanged(): return (lax.ppermute(high, axis, up), lax.ppermute(low, axis, down))  13.7 us
    ppermute x3, waiting for transfers between devices, on_device(): lax.ppermute(pieces[k], 'depth', [(i, (i + 2 * k) % 8) for i in range(8)])  11.4 us
    ppermute x4, waiting for transfers between devices, exchanged(): return (lax.ppermute(high, axis, up), lax.ppermute(low, axis, down))  9.69 us
    pallas_call x1, Pallas kernels, index_call(): pl.pallas_call(index_kernel, in_specs=[SMEM, VMEM, VMEM], out_specs=[VMEM...  8.88 us
    pallas_call x1, Pallas kernels, on_device(): pl.pallas_call(conv_kernel, in_specs=[SMEM] + [VMEM] * 7, out_specs=VMEM,...  7.44 us
    ppermute x3, starting transfers between devices, on_device(): lax.ppermute(pieces[k], 'depth', [(i, (i + 2 * k) % 8) for i in range(8)])  4.08 us
  transfers between devices with their start and end apart: 8, of which 7 were waited for; matrix products, arithmetic and copies ran while one was open for 0% of the time, Pallas kernels for 0%

profile of v1, /device:TPU:41, one launch (start us, length us, event | category | flops | bytes accessed | tf_op | source)
XLA Modules:
  0.0 135.7 jit_solution(6465787930129515698)
XLA Ops:
  0.7 1.6 %copy.17 = f32[5120,8]{1,0:T(8,128)S(1)} copy(f32[5120,8]{0,1:T(8,128)} %bitcast.58) | data formatting | bytes 327680 | tf_op jit(solution)/shard_map/transpose | solution.py:431
  2.4 2.2 %reshape.49.gap_ref = f32[160,256]{1,0:T(8,128)} reshape(f32[5120,8]{1,0:T(8,128)S(1)} %copy.17) | data formatting | bytes 327680 | tf_op jit(solution)/shard_map/reshape | solution.py:431
  4.6 0.7 fusion.4
  5.4 0.6 pad_add_fusion.where_ref
  5.9 8.9 %index.1 = (s32[40,128]{1,0:T(8,128)}, f32[4,2,8,128]{3,2,1,0:T(8,128)}) custom-call(s32[3]{0:T(128)} %pad_add_fusion.where_ref, s32[64,128]{1,0:T(8,128)} %bitcast.65, s32[40,128]{1,0:T(8,128)} %bitcast.66), custom_call_target="tpu_custom_call" | custom-call | tf_op jit(solution)/shard_map/index/pallas_call | solution.py:400
  14.9 0.6 pad_maximum_fusion.1.wd_ref
  15.5 0.6 tile.15
  16.6 34.8 %segments.1 = (bf16[4,1040,128]{2,1,0:T(8,128)(2,1)}, bf16[4,1040,128]{2,1,0:T(8,128)(2,1)}) custom-call(s32[5120]{0:T(1024)} %bitcast.59, s32[1]{0:T(128)} %bitcast.51.live_smem, bf16[40960,128]{1,0:T(8,128)(2,1)} %bitcast.52, f32[160,256]{1,0:T(8,128)} %reshape.49.gap_ref, s32[40,128]{1,0:T(8,128)} %get-tuple-element.13.pos_ref, ...), custom_call_target="tpu_custom_call" | custom-call | tf_op jit(solution)/shard_map/segments/pallas_call | solution.py:312
  51.5 0.7 collective-permute-start
  52.1 2.5 %collective-permute-done.arrived_ref = bf16[4,1040,128]{2,1,0:T(8,128)(2,1)S(1)} collective-permute-done((bf16[4,1040,128]{2,1,0:T(8,128)(2,1)}, bf16[4,1040,128]{2,1,0:T(8,128)(2,1)S(1)}, u32[]{:S(2)}, u32[]{:S(2)}) %collective-permute-start) | collective-permute-done | bytes 1064992 | tf_op jit(solution)/shard_map/ppermute | solution.py:444
  54.7 1.0 copy-done.1
  55.6 3.8 %pair.1 = (bf16[1040,128]{1,0:T(8,128)(2,1)}, bf16[1040,128]{1,0:T(8,128)(2,1)}, bf16[1040,128]{1,0:T(8,128)(2,1)}, bf16[1040,128]{1,0:T(8,128)(2,1)}) custom-call(s32[3]{0:T(128)} %pad_add_fusion.where_ref, bf16[4,1040,128]{2,1,0:T(8,128)(2,1)} %get-tuple-element.14.near_ref, bf16[4,1040,128]{2,1,0:T(8,128)(2,1)} %copy-done.1), custom_call_target="tpu_custom_call" | custom-call | tf_op jit(solution)/shard_map/pair/pallas_call | solution.py:446
  59.4 1.3 collective-permute-start.1
  60.7 0.7 collective-permute-start.2
  61.4 2.1 %collective-permute-start.3 = (bf16[1040,128]{1,0:T(8,128)(2,1)}, bf16[1040,128]{1,0:T(8,128)(2,1)S(1)}, u32[]{:S(2)}, u32[]{:S(2)}) collective-permute-start(bf16[1040,128]{1,0:T(8,128)(2,1)} %get-tuple-element.19), channel_id=1, source_target_pairs={{0,192},{32,224},{64,0},{96,32},{128,64},{160,96},{192,128},{224,1... | collective-permute-start | bytes 798728 | tf_op jit(solution)/shard_map/ppermute | solution.py:454
  63.5 3.7 %collective-permute-done.1.p1_ref = bf16[1040,128]{1,0:T(8,128)(2,1)S(1)} collective-permute-done((bf16[1040,128]{1,0:T(8,128)(2,1)}, bf16[1040,128]{1,0:T(8,128)(2,1)S(1)}, u32[]{:S(2)}, u32[]{:S(2)}) %collective-permute-start.1) | collective-permute-done | bytes 266272 | tf_op jit(solution)/shard_map/ppermute | solution.py:454
  67.2 2.6 %collective-permute-done.2.p2_ref = bf16[1040,128]{1,0:T(8,128)(2,1)S(1)} collective-permute-done((bf16[1040,128]{1,0:T(8,128)(2,1)}, bf16[1040,128]{1,0:T(8,128)(2,1)S(1)}, u32[]{:S(2)}, u32[]{:S(2)}) %collective-permute-start.2) | collective-permute-done | bytes 266272 | tf_op jit(solution)/shard_map/ppermute | solution.py:454
  69.8 5.1 %collective-permute-done.3.p3_ref = bf16[1040,128]{1,0:T(8,128)(2,1)S(1)} collective-permute-done((bf16[1040,128]{1,0:T(8,128)(2,1)}, bf16[1040,128]{1,0:T(8,128)(2,1)S(1)}, u32[]{:S(2)}, u32[]{:S(2)}) %collective-permute-start.3) | collective-permute-done | bytes 266272 | tf_op jit(solution)/shard_map/ppermute | solution.py:454
  74.9 0.7 copy-done.4
  75.6 2.7 %merge.1 = bf16[32,40,128]{2,1,0:T(8,128)(2,1)} custom-call(s32[3]{0:T(128)} %pad_add_fusion.where_ref, bf16[1040,128]{1,0:T(8,128)(2,1)} %get-tuple-element.16.p0_ref, bf16[1040,128]{1,0:T(8,128)(2,1)} %copy-done.2, bf16[1040,128]{1,0:T(8,128)(2,1)} %copy-done.3, bf16[1040,128]{1,0:T(8,128)(2,1)} %copy-done.4, f32[4,2,8,128]{3,2,1,0:T(8,128)} %get-tuple-element.20.info_ref), custom_call_target="tpu_custom_call" | custom-call | tf_op jit(solution)/shard_map/merge/pallas_call | solution.py:457
  78.3 21.7 %all_to_all.5.in_ref = bf16[32,40,128]{2,1,0:T(8,128)(2,1)} all-to-all(bf16[32,40,128]{2,1,0:T(8,128)(2,1)} %merge.1), channel_id=1, replica_groups=mesh['depth'=8,'rays'=32] {'rays'}, dimensions={0} | all-to-all | bytes 655360 | tf_op jit(solution)/shard_map/all_to_all | solution.py:464
  100.0 2.4 %place.1 = bf16[1024,128]{1,0:T(8,128)(2,1)} custom-call(bf16[32,40,128]{2,1,0:T(8,128)(2,1)} %all_to_all.5.in_ref), custom_call_target="tpu_custom_call" | custom-call | tf_op jit(solution)/shard_map/place/pallas_call | solution.py:465
  102.4 0.8 fusion.8
  103.2 6.4 %collective-permute-start.4 = (bf16[16,8,128]{2,1,0:T(8,128)(2,1)S(1)}, bf16[16,8,128]{2,1,0:T(8,128)(2,1)S(1)}, u32[]{:S(2)}, u32[]{:S(2)}) collective-permute-start(bf16[16,8,128]{2,1,0:T(8,128)(2,1)S(1)} %get-tuple-element.23), channel_id=1, source_target_pairs={{0,32},{32,64},{64,96},{96,128},{128,160},{160,192},{192,224},{1,3... | collective-permute-start | bytes 98312 | tf_op jit(solution)/shard_map/ppermute | solution.py:356
  109.6 1.9 %collective-permute-start.5 = (bf16[16,8,128]{2,1,0:T(8,128)(2,1)S(1)}, bf16[16,8,128]{2,1,0:T(8,128)(2,1)S(1)}, u32[]{:S(2)}, u32[]{:S(2)}) collective-permute-start(bf16[16,8,128]{2,1,0:T(8,128)(2,1)S(1)} %get-tuple-element.24), channel_id=1, source_target_pairs={{32,0},{64,32},{96,64},{128,96},{160,128},{192,160},{224,192},{33,... | collective-permute-start | bytes 98312 | tf_op jit(solution)/shard_map/ppermute | solution.py:356
  111.5 3.3 %collective-permute-done.5 = bf16[16,8,128]{2,1,0:T(8,128)(2,1)S(1)} collective-permute-done((bf16[16,8,128]{2,1,0:T(8,128)(2,1)S(1)}, bf16[16,8,128]{2,1,0:T(8,128)(2,1)S(1)}, u32[]{:S(2)}, u32[]{:S(2)}) %collective-permute-start.5) | collective-permute-done | bytes 32800 | tf_op jit(solution)/shard_map/ppermute | solution.py:356
  114.8 1.0 pad_maximum_fusion
  115.8 3.5 %collective-permute-start.7 = (bf16[4,80,128]{2,1,0:T(8,128)(2,1)S(1)}, bf16[4,80,128]{2,1,0:T(8,128)(2,1)S(1)}, u32[]{:S(2)}, u32[]{:S(2)}) collective-permute-start(bf16[4,80,128]{2,1,0:T(8,128)(2,1)S(1)} %get-tuple-element.21), channel_id=1, source_target_pairs={{1,0},{2,1},{3,2},{4,3},{5,4},{6,5},{7,6},{8,7},{9,8},{10,9},{11,1... | collective-permute-start | bytes 245768 | tf_op jit(solution)/shard_map/ppermute | solution.py:356
  119.3 1.9 %collective-permute-start.6 = (bf16[4,80,128]{2,1,0:T(8,128)(2,1)S(1)}, bf16[4,80,128]{2,1,0:T(8,128)(2,1)S(1)}, u32[]{:S(2)}, u32[]{:S(2)}) collective-permute-start(bf16[4,80,128]{2,1,0:T(8,128)(2,1)S(1)} %get-tuple-element.22), channel_id=1, source_target_pairs={{0,1},{1,2},{2,3},{3,4},{4,5},{5,6},{6,7},{7,8},{8,9},{9,10},{10,1... | collective-permute-start | bytes 245768 | tf_op jit(solution)/shard_map/ppermute | solution.py:356
  121.5 6.1 %collective-permute-done.6 = bf16[4,80,128]{2,1,0:T(8,128)(2,1)S(1)} collective-permute-done((bf16[4,80,128]{2,1,0:T(8,128)(2,1)S(1)}, bf16[4,80,128]{2,1,0:T(8,128)(2,1)S(1)}, u32[]{:S(2)}, u32[]{:S(2)}) %collective-permute-start.6) | collective-permute-done | bytes 81952 | tf_op jit(solution)/shard_map/ppermute | solution.py:356
  127.7 0.6 copy-done.6
  128.3 7.4 %conv.1 = bf16[16,64,128]{2,1,0:T(8,128)(2,1)} custom-call(s32[3]{0:T(128)} %pad_add_fusion.where_ref, bf16[1280,128]{1,0:T(8,128)(2,1)} %bitcast.53, bf16[320,128]{1,0:T(8,128)(2,1)} %bitcast.61, bf16[320,128]{1,0:T(8,128)(2,1)} %bitcast.60, bf16[5,640,128]{2,1,0:T(8,128)(2,1)} %bitcast.56, f32[1,128]{1,0:T(1,128)} %bitcast.69, ...), custom_call_target="tpu_custom_call" | custom-call | tf_op jit(solution)/shard_map/conv/pallas_call | solution.py:476
  (30 shorter events, 1.0 us)
Async XLA Ops:
  2.3 2.3 %copy-start.7 = (bf16[1,128,128]{2,1,0:T(8,128)(2,1)S(1)}, bf16[1,128,128]{2,1,0:T(8,128)(2,1)}, u32[]{:S(2)}) copy-start(bf16[1,128,128]{2,1,0:T(8,128)(2,1)} %param.20) | copy-start | bytes 98308
  2.3 2.3 %copy-start.8 = (bf16[1,128,128]{2,1,0:T(8,128)(2,1)S(1)}, bf16[1,128,128]{2,1,0:T(8,128)(2,1)}, u32[]{:S(2)}) copy-start(bf16[1,128,128]{2,1,0:T(8,128)(2,1)} %param.22) | copy-start | bytes 98308
  2.4 12.4 %copy-start.9 = (bf16[1,128]{1,0:T(2,128)(2,1)S(1)}, bf16[1,128]{1,0:T(2,128)(2,1)}, u32[]{:S(2)}) copy-start(bf16[1,128]{1,0:T(2,128)(2,1)} %param.24) | copy-start | bytes 772
  2.4 13.2 %copy-start.10 = (f32[1,128]{1,0:T(1,128)S(1)}, f32[1,128]{1,0:T(1,128)}, u32[]{:S(2)}) copy-start(f32[1,128]{1,0:T(1,128)} %param.21) | copy-start | bytes 1540
  2.4 13.7 %copy-start.11 = (f32[1,128]{1,0:T(1,128)S(1)}, f32[1,128]{1,0:T(1,128)}, u32[]{:S(2)}) copy-start(f32[1,128]{1,0:T(1,128)} %param.23) | copy-start | bytes 1540
  51.5 3.2 %collective-permute-start = (bf16[4,1040,128]{2,1,0:T(8,128)(2,1)}, bf16[4,1040,128]{2,1,0:T(8,128)(2,1)S(1)}, u32[]{:S(2)}, u32[]{:S(2)}) collective-permute-start(bf16[4,1040,128]{2,1,0:T(8,128)(2,1)} %get-tuple-element.15), channel_id=1, source_target_pairs={{0,32},{32,0},{64,96},{96,64},{128,160},{160,128},{192,224},{224,1... | collective-permute-start | bytes 3194888 | tf_op jit(solution)/shard_map/ppermute | solution.py:444
  54.7 1.0 copy-start.1
  59.4 7.8 %collective-permute-start.1 = (bf16[1040,128]{1,0:T(8,128)(2,1)}, bf16[1040,128]{1,0:T(8,128)(2,1)S(1)}, u32[]{:S(2)}, u32[]{:S(2)}) collective-permute-start(bf16[1040,128]{1,0:T(8,128)(2,1)} %get-tuple-element.17), channel_id=1, source_target_pairs={{0,64},{32,96},{64,128},{96,160},{128,192},{160,224},{192,0},{224,... | collective-permute-start | bytes 798728 | tf_op jit(solution)/shard_map/ppermute | solution.py:454
  60.7 9.1 %collective-permute-start.2 = (bf16[1040,128]{1,0:T(8,128)(2,1)}, bf16[1040,128]{1,0:T(8,128)(2,1)S(1)}, u32[]{:S(2)}, u32[]{:S(2)}) collective-permute-start(bf16[1040,128]{1,0:T(8,128)(2,1)} %get-tuple-element.18), channel_id=1, source_target_pairs={{0,128},{32,160},{64,192},{96,224},{128,0},{160,32},{192,64},{224,... | collective-permute-start | bytes 798728 | tf_op jit(solution)/shard_map/ppermute | solution.py:454
  61.4 13.4 %collective-permute-start.3 = (bf16[1040,128]{1,0:T(8,128)(2,1)}, bf16[1040,128]{1,0:T(8,128)(2,1)S(1)}, u32[]{:S(2)}, u32[]{:S(2)}) collective-permute-start(bf16[1040,128]{1,0:T(8,128)(2,1)} %get-tuple-element.19), channel_id=1, source_target_pairs={{0,192},{32,224},{64,0},{96,32},{128,64},{160,96},{192,128},{224,1... | collective-permute-start | bytes 798728 | tf_op jit(solution)/shard_map/ppermute | solution.py:454
  67.2 7.7 %copy-start.2 = (bf16[1040,128]{1,0:T(8,128)(2,1)}, bf16[1040,128]{1,0:T(8,128)(2,1)S(1)}, u32[]{:S(2)}) copy-start(bf16[1040,128]{1,0:T(8,128)(2,1)S(1)} %collective-permute-done.1.p1_ref) | copy-start | bytes 798724
  69.8 5.1 %copy-start.3 = (bf16[1040,128]{1,0:T(8,128)(2,1)}, bf16[1040,128]{1,0:T(8,128)(2,1)S(1)}, u32[]{:S(2)}) copy-start(bf16[1040,128]{1,0:T(8,128)(2,1)S(1)} %collective-permute-done.2.p2_ref) | copy-start | bytes 798724
  74.9 0.7 copy-start.4
  103.2 8.3 %collective-permute-start.4 = (bf16[16,8,128]{2,1,0:T(8,128)(2,1)S(1)}, bf16[16,8,128]{2,1,0:T(8,128)(2,1)S(1)}, u32[]{:S(2)}, u32[]{:S(2)}) collective-permute-start(bf16[16,8,128]{2,1,0:T(8,128)(2,1)S(1)} %get-tuple-element.23), channel_id=1, source_target_pairs={{0,32},{32,64},{64,96},{96,128},{128,160},{160,192},{192,224},{1,3... | collective-permute-start | bytes 98312 | tf_op jit(solution)/shard_map/ppermute | solution.py:356
  109.6 5.2 %collective-permute-start.5 = (bf16[16,8,128]{2,1,0:T(8,128)(2,1)S(1)}, bf16[16,8,128]{2,1,0:T(8,128)(2,1)S(1)}, u32[]{:S(2)}, u32[]{:S(2)}) collective-permute-start(bf16[16,8,128]{2,1,0:T(8,128)(2,1)S(1)} %get-tuple-element.24), channel_id=1, source_target_pairs={{32,0},{64,32},{96,64},{128,96},{160,128},{192,160},{224,192},{33,... | collective-permute-start | bytes 98312 | tf_op jit(solution)/shard_map/ppermute | solution.py:356
  115.8 11.9 %copy-start = (bf16[16,80,128]{2,1,0:T(8,128)(2,1)}, bf16[16,80,128]{2,1,0:T(8,128)(2,1)S(1)}, u32[]{:S(2)}) copy-start(bf16[16,80,128]{2,1,0:T(8,128)(2,1)S(1)} %pad_maximum_fusion) | copy-start | bytes 983044
  115.8 5.7 %collective-permute-start.7 = (bf16[4,80,128]{2,1,0:T(8,128)(2,1)S(1)}, bf16[4,80,128]{2,1,0:T(8,128)(2,1)S(1)}, u32[]{:S(2)}, u32[]{:S(2)}) collective-permute-start(bf16[4,80,128]{2,1,0:T(8,128)(2,1)S(1)} %get-tuple-element.21), channel_id=1, source_target_pairs={{1,0},{2,1},{3,2},{4,3},{5,4},{6,5},{7,6},{8,7},{9,8},{10,9},{11,1... | collective-permute-start | bytes 245768 | tf_op jit(solution)/shard_map/ppermute | solution.py:356
  119.3 8.3 %collective-permute-start.6 = (bf16[4,80,128]{2,1,0:T(8,128)(2,1)S(1)}, bf16[4,80,128]{2,1,0:T(8,128)(2,1)S(1)}, u32[]{:S(2)}, u32[]{:S(2)}) collective-permute-start(bf16[4,80,128]{2,1,0:T(8,128)(2,1)S(1)} %get-tuple-element.22), channel_id=1, source_target_pairs={{0,1},{1,2},{2,3},{3,4},{4,5},{5,6},{6,7},{7,8},{8,9},{9,10},{10,1... | collective-permute-start | bytes 245768 | tf_op jit(solution)/shard_map/ppermute | solution.py:356
  121.5 6.1 %copy-start.5 = (bf16[4,80,128]{2,1,0:T(8,128)(2,1)}, bf16[4,80,128]{2,1,0:T(8,128)(2,1)S(1)}, u32[]{:S(2)}) copy-start(bf16[4,80,128]{2,1,0:T(8,128)(2,1)S(1)} %collective-permute-done.7) | copy-start | bytes 245764
  127.6 0.6 copy-start.6

commit v2 on v1

v2 whole, which is shorter than its diff:
```python
import functools

import jax
import jax.numpy as jnp
from jax import lax
from jax.experimental import pallas as pl
from jax.experimental.pallas import tpu as pltpu
from jax.sharding import PartitionSpec as P

FEAT = 128
SAMPLES = 8
TH = 16
TW = 64
WIDE = 512
HEIGHT = 512
SLOTS = 5120
RAYS = 8192
LANES = 128
HALO = 4
PITCH = TW + 16
PAIR_ORDER = (2, 1, 3, 0)
PIECE = 1024
PACK = PIECE + 16
SUPER = 256
f32 = jnp.float32
bf16 = jnp.bfloat16
i32 = jnp.int32


def dot_nt(lhs, rhs):
    return lax.dot_general(lhs, rhs, (((1,), (1,)), ((), ())), preferred_element_type=f32)


def dot_nn(lhs, rhs):
    return jnp.dot(lhs, rhs, preferred_element_type=f32)


def iota(shape, axis):
    return lax.broadcasted_iota(i32, shape, axis)


def as_bf16(mask):
    return jnp.where(mask, 1.0, 0.0).astype(bf16)


def coordinates():
    place = lax.axis_index("depth")
    return place & 1, place >> 1, lax.axis_index("rays")


def rank_sum(parts):
    total = parts[0]
    for part in parts[1:]:
        total = total + part
    return jnp.sum(total, axis=0, keepdims=True)


def index_rays(pixel_ref, ids_ref, pos_ref, ray_ref):
    my_core, my_y, _ = coordinates()
    pixel = pixel_ref[...]
    row, col = pixel >> 9, pixel & (WIDE - 1)
    block_col = col >> 6
    core_rel = (block_col & 1) ^ my_core
    y_rel = ((block_col >> 1) - my_y) & 3
    group = core_rel * 128 + y_rel * 32 + (row >> 4)
    column = group.astype(f32).T.astype(i32)
    earlier = iota((LANES, LANES), 0) < iota((LANES, LANES), 1)
    iota16 = iota((16, LANES), 0)
    seen = jnp.zeros((16, 16), f32)
    ranks = []
    for j in range(RAYS // LANES):
        g = group[j : j + 1, :]
        same = jnp.where((column[:, j : j + 1] == g) & earlier, 1.0, 0.0)
        coarse = as_bf16(iota16 == (g >> 4))
        fine = iota16 == (g & 15)
        found = jnp.where(fine, dot_nn(seen.astype(bf16), coarse), 0.0)
        seen = seen + dot_nt(as_bf16(fine), coarse)
        parts = [same[8 * k : 8 * k + 8] for k in range(16)] + [found[:8], found[8:]]
        ranks.append(rank_sum(parts))
    rank = jnp.concatenate(ranks, axis=0).astype(i32)
    high = group >> 2
    low = (group & 3) * 32 + rank
    ray_ref[...] = high * LANES + low
    table = jnp.concatenate(
        [(high * LANES).astype(f32).T, low.astype(f32).T], axis=1
    ).astype(bf16)
    high_iota = iota((RAYS // LANES, LANES), 0)
    lane_iota = iota((LANES, LANES), 0)
    for j in range(SLOTS // LANES):
        ids = ids_ref[j : j + 1, :]
        hot = as_bf16(high_iota == (ids >> 7))
        found = dot_nn(table, jnp.concatenate([hot, hot], axis=0))
        found = jnp.where(lane_iota == (ids & (LANES - 1)), found, 0.0)
        pos_ref[j : j + 1, :] = rank_sum([found[8 * k : 8 * k + 8] for k in range(16)]).astype(i32)


def arrange_taps(k1_ref, k2_ref, main1, main2):
    for k_ref, main in ((k1_ref, main1), (k2_ref, main2)):
        for i in range(4):
            down, right = (i // 2) * 5 * FEAT, (i % 2) * FEAT
            main[down : down + 5 * FEAT, right : right + FEAT] = k_ref[i]


def info_kernel(pixel_ref, ray_ref, k1_ref, k2_ref, info_ref, main1, main2):
    arrange_taps(k1_ref, k2_ref, main1, main2)
    _, _, bundle = coordinates()
    pixel = pixel_ref[...]
    local_row = ((pixel >> 9) & (TH - 1)).astype(f32)
    local_col = (pixel & (TW - 1)).astype(f32)
    ray = ray_ref[...]
    lane_iota = iota((LANES, LANES), 0)
    iota8 = iota((8, LANES), 0)
    own = jnp.zeros((16, LANES), f32)
    for j in range(RAYS // LANES):
        at = ray[j : j + 1, :]
        mine = iota8 == (at >> 7)
        values = jnp.concatenate(
            [
                jnp.where(mine, local_row[j : j + 1, :], 0.0),
                jnp.where(mine, local_col[j : j + 1, :], 0.0),
            ],
            axis=0,
        ).astype(bf16)
        own = own + dot_nt(values, as_bf16(lane_iota == (at & (LANES - 1))))
    quarter = bundle & 3
    keep = (iota((16, LANES), 1) >> 5) == quarter
    for q in range(4):
        shift = ((quarter - q) & 3) * 32
        info_ref[q] = jnp.where(keep, pltpu.roll(own, shift, 1), 0.0)


def segment_kernel(
    live_smem,
    enc_ref,
    gap_ref,
    pixel_ref,
    ids_ref,
    w1_ref,
    b1_ref,
    w2_ref,
    b2_ref,
    wd_ref,
    wf_ref,
    near_hbm,
    far_hbm,
    ray_ref,
    spread,
    hidden,
    first_a,
    first_b,
    wide1,
    wide2,
    pre,
    depth,
    colour_a,
    colour_b,
    table_ref,
    pos_ref,
    pos_smem,
    staged,
    pos_sem,
    out_sems,
):
    step = pl.program_id(0)
    to_smem = pltpu.make_async_copy(pos_ref, pos_smem, pos_sem)
    half = SUPER * SAMPLES // 2

    @pl.when(step == 0)
    def _():
        zero = jnp.zeros((FEAT, FEAT), bf16)
        for wide, w in ((wide1, w1_ref), (wide2, w2_ref)):
            wide[:FEAT, :FEAT] = w[0]
            wide[:FEAT, FEAT:] = zero
            wide[FEAT:, :FEAT] = zero
            wide[FEAT:, FEAT:] = w[0]
        index_rays(pixel_ref, ids_ref, pos_ref, ray_ref)
        to_smem.start()

    bias1 = jnp.concatenate([b1_ref[...]] * 2, axis=1)
    bias2 = jnp.concatenate([b2_ref[...]] * 2, axis=1)
    head = wd_ref[...].astype(f32)
    lane8 = iota((SAMPLES, LANES), 1)
    chunk = RAYS // (SLOTS // SUPER * 4) * 8 + 8
    start = pl.multiple_of(jnp.minimum(step * chunk, RAYS - chunk), 8)
    spread[pl.ds(start, chunk), :] = jnp.zeros((chunk, FEAT), f32)

    def layer_one(base, out):
        x = jnp.concatenate(
            [enc_ref[base : base + half, :], enc_ref[base + half : base + 2 * half, :]], axis=1
        )
        out[...] = jnp.maximum((dot_nn(x, wide1[...]) + bias1).astype(bf16), 0.0)

    def layer_two(source, block):
        h2 = jnp.maximum(dot_nn(source[...], wide2[...]) + bias2, 0.0)
        hidden[pl.ds(pl.multiple_of(block * half, half), half), :] = h2.astype(bf16)
        for side in range(2):
            part = h2[:, side * FEAT : (side + 1) * FEAT] * head
            total = jnp.sum(part, axis=1, keepdims=True)
            lined = jnp.zeros((SAMPLES, LANES), f32)
            for s in range(LANES):
                lined = jnp.where(lane8 == s, total[SAMPLES * s : SAMPLES * (s + 1), :], lined)
            pre[2 * block + side] = lined

    layer_two(first_b, jnp.maximum(2 * step - 1, 0))
    layer_one(0, first_a)
    layer_two(first_a, 2 * step)
    layer_one(SUPER * SAMPLES, first_b)

    @pl.when(step == pl.num_programs(0) - 1)
    def _():
        live = live_smem[0]
        blocks = SLOTS // SUPER
        layer_two(first_b, blocks - 1)
        to_smem.wait()
        sample = iota((SAMPLES, LANES), 0)
        for b in range(SLOTS // LANES):
            v = pre[b]
            soft = jnp.maximum(v, 0.0) + jnp.log1p(jnp.exp(-jnp.abs(v)))
            opacity = soft * gap_ref[:, b * LANES : (b + 1) * LANES]
            inc = opacity
            for shift in (1, 2, 4):
                inc = inc + jnp.where(sample >= shift, pltpu.roll(inc, shift, 0), 0.0)
            weight = jnp.exp(opacity - inc) * (1.0 - jnp.exp(-opacity))
            alive = b * LANES + lane8 < live
            pre[b] = jnp.where(alive, weight, 0.0)
            depth[b : b + 1, :] = jnp.where(alive, inc, 0.0)[SAMPLES - 1 :, :]
        high_iota, low_iota = iota((RAYS // LANES, LANES), 0), iota((LANES, LANES), 0)

        def depth_table(block, table):
            for h in range(2):
                at = pos_ref[pl.ds(2 * block + h, 1), :]
                here = depth[pl.ds(2 * block + h, 1), :]
                coarse = here.astype(bf16).astype(f32)
                high = high_iota == (at >> 7)
                wanted = jnp.concatenate(
                    [jnp.where(high, coarse, 0.0), jnp.where(high, here - coarse, 0.0)], axis=0
                ).astype(bf16)
                table = table + dot_nt(wanted, as_bf16(low_iota == (at & (LANES - 1))))
            return table

        of_slot = iota((32, SUPER), 0) == (iota((32, SUPER), 1) >> 3)
        of_sample = as_bf16(iota((SAMPLES, SUPER), 0) == (iota((SAMPLES, SUPER), 1) & 7))

        def mix(block, colour):
            spaced = [
                lax.dot_general(
                    pre[2 * block + side].astype(bf16),
                    of_sample,
                    (((0,), (0,)), ((), ())),
                    preferred_element_type=f32,
                )
                for side in range(2)
            ]
            gathered = [None] * 8
            for i in range(4):
                rows = slice(32 * i, 32 * i + 32)
                both = jnp.concatenate(
                    [jnp.where(of_slot, spaced[side][rows], 0.0) for side in range(2)], axis=0
                ).astype(bf16)
                at = block * half + i * SUPER
                summed = dot_nn(both, hidden[pl.ds(at, SUPER), :])
                gathered[i] = summed[:32, :FEAT]
                gathered[i + 4] = summed[32:, FEAT:]
            mixed = jnp.concatenate(gathered, axis=0).astype(bf16)
            colour[...] = dot_nn(mixed, wf_ref[0])

        def scatter(block, colour):
            for s in range(SUPER):
                slot = block * SUPER + s
                at = pos_smem[slot // LANES, slot % LANES]
                spread[pl.ds(at, 1), :] = colour[s : s + 1, :]

        mix(0, colour_a)

        table_ref[...] = jnp.zeros_like(table_ref)
        for t in range(blocks // 2):

            @pl.when(live >= 0)
            def _(t=t):
                table = table_ref[...]
                mix(2 * t + 1, colour_b)
                scatter(2 * t, colour_a)
                table = depth_table(2 * t, table)
                if 2 * t + 2 < blocks:
                    mix(2 * t + 2, colour_a)
                scatter(2 * t + 1, colour_b)
                table_ref[...] = depth_table(2 * t + 1, table)

        table = table_ref[...]
        stores = []
        for n in range(8):
            k, g = 1 - n // 4, n % 4
            at = (4 * k + g) * PIECE
            staged[n, :PIECE, :] = spread[at : at + PIECE, :].astype(bf16)
            rows = (4 * k + g) * 8
            staged[n, PIECE:, :] = jnp.concatenate(
                [table[rows : rows + 8], table[64 + rows : 72 + rows]], axis=0
            ).astype(bf16)
            out = (near_hbm, far_hbm)[k].at[g]
            stores.append(pltpu.make_async_copy(staged.at[n], out, out_sems.at[n]))
            stores[-1].start()
        for store in stores:
            store.wait()


def read_depth(ref):
    rows = ref[PIECE:, :].astype(f32)
    return rows[:8] + rows[8:]


def scaled(ref, factors, i):
    return ref[i * LANES : (i + 1) * LANES, :].astype(f32) * factors[:, i : i + 1]


def pair_kernel(mine_hbm, arrived_hbm, o0, o1, o2, o3, mine, arrived, done, in_sems, out_sems):
    my_core, _, _ = coordinates()
    loads = [
        (
            pltpu.make_async_copy(mine_hbm.at[g], mine.at[g], in_sems.at[2 * g]),
            pltpu.make_async_copy(arrived_hbm.at[g], arrived.at[g], in_sems.at[2 * g + 1]),
        )
        for g in PAIR_ORDER
    ]
    for two in loads:
        for load in two:
            load.start()

    def combine(front_all, back_all):
        stores = []
        for g, two in zip(PAIR_ORDER, loads):
            for load in two:
                load.wait()
            front, back, out = front_all.at[g], back_all.at[g], done.at[g]
            d_front, d_back = read_depth(front), read_depth(back)
            fade = jnp.exp(-d_front).T
            for i in range(8):
                at = slice(i * LANES, (i + 1) * LANES)
                out[at, :] = (front[at, :].astype(f32) + scaled(back, fade, i)).astype(bf16)
            both = d_front + d_back
            coarse = both.astype(bf16).astype(f32)
            out[PIECE:, :] = jnp.concatenate([coarse, both - coarse], axis=0).astype(bf16)
            store = pltpu.make_async_copy(out, (o0, o1, o2, o3)[g], out_sems.at[g])
            store.start()
            stores.append(store)
        for store in stores:
            store.wait()

    @pl.when(my_core == 0)
    def _():
        combine(mine, arrived)

    @pl.when(my_core == 1)
    def _():
        combine(arrived, mine)


def merge_kernel(p0_ref, p1_ref, p2_ref, p3_ref, info_ref, out_ref):
    _, y, _ = coordinates()
    pieces = (p0_ref, p1_ref, p2_ref, p3_ref)
    places = [(y - k) & 3 for k in range(4)]
    depths = [read_depth(ref) for ref in pieces]
    factors = []
    for a in range(4):
        before = jnp.zeros_like(depths[0])
        for b in range(4):
            if b != a:
                before = before + jnp.where(places[b] < places[a], depths[b], 0.0)
        factors.append(jnp.exp(-before).T)
    for i in range(8):
        total = scaled(pieces[0], factors[0], i)
        for k in range(1, 4):
            total = total + scaled(pieces[k], factors[k], i)
        total = total.astype(bf16)
        for q in range(4):
            tile = i * 4 + q
            out_ref[tile, :32, :] = total[q * 32 : q * 32 + 32, :]
            extra = jnp.concatenate(
                [
                    info_ref[q, i : i + 1, :],
                    info_ref[q, i + 8 : i + 9, :],
                    jnp.zeros((6, LANES), f32),
                ],
                axis=0,
            )
            out_ref[tile, 32:, :] = extra.astype(bf16)


def place_kernel(in_ref, out_ref, left_ref, right_ref):
    total = jnp.zeros((TH * TW, FEAT), f32)
    pixel_iota = iota((TH * TW, LANES), 0)
    for g in range(8):
        rows = jnp.concatenate([in_ref[4 * g + q, :32, :] for q in range(4)], axis=0)
        place = in_ref[4 * g, 32:, :].astype(f32)
        for q in range(1, 4):
            place = place + in_ref[4 * g + q, 32:, :].astype(f32)
        pixel = (place[0:1, :] * TW + place[1:2, :]).astype(i32)
        total = total + dot_nn(as_bf16(pixel_iota == pixel), rows)
    out_ref[...] = total.astype(bf16)
    left_ref[...] = jnp.concatenate([total[y * TW : y * TW + 8] for y in range(TH)]).astype(bf16)
    right_ref[...] = jnp.concatenate(
        [total[y * TW + TW - 8 : y * TW + TW] for y in range(TH)]
    ).astype(bf16)


def whole(shape):
    return pl.BlockSpec(shape, lambda *_: (0,) * len(shape))


def shape_of(shape, dtype):
    return jax.ShapeDtypeStruct(shape, dtype)


VMEM = pl.BlockSpec(memory_space=pltpu.VMEM)
HBM = pl.BlockSpec(memory_space=pltpu.HBM)


def segments(live, enc, gaps, pixel, ids, w1, b1, w2, b2, wd, wf):
    rows = 2 * SUPER * SAMPLES
    out = shape_of((4, PACK, FEAT), bf16)
    return pl.pallas_call(
        segment_kernel,
        grid_spec=pltpu.PrefetchScalarGridSpec(
            num_scalar_prefetch=1,
            grid=(SLOTS * SAMPLES // rows,),
            in_specs=[pl.BlockSpec((rows, FEAT), lambda i, *_: (i, 0))]
            + [whole(a.shape) for a in (gaps, pixel, ids, w1, b1, w2, b2, wd, wf)],
            out_specs=[HBM, HBM, whole(pixel.shape)],
            scratch_shapes=[
                pltpu.VMEM((RAYS, FEAT), f32),
                pltpu.VMEM((SLOTS * SAMPLES // 2, 2 * FEAT), bf16),
                pltpu.VMEM((SUPER * SAMPLES // 2, 2 * FEAT), bf16),
                pltpu.VMEM((SUPER * SAMPLES // 2, 2 * FEAT), bf16),
                pltpu.VMEM((2 * FEAT, 2 * FEAT), bf16),
                pltpu.VMEM((2 * FEAT, 2 * FEAT), bf16),
                pltpu.VMEM((SLOTS // LANES, SAMPLES, LANES), f32),
                pltpu.VMEM((SLOTS // LANES, LANES), f32),
                pltpu.VMEM((SUPER, FEAT), f32),
                pltpu.VMEM((SUPER, FEAT), f32),
                pltpu.VMEM((2 * RAYS // LANES, LANES), f32),
                pltpu.VMEM((SLOTS // LANES, LANES), i32),
                pltpu.SMEM((SLOTS // LANES, LANES), i32),
                pltpu.VMEM((8, PACK, FEAT), bf16),
                pltpu.SemaphoreType.DMA,
                pltpu.SemaphoreType.DMA((8,)),
            ],
        ),
        out_shape=[out, out, shape_of(pixel.shape, i32)],
        name="segments",
    )(live, enc, gaps, pixel, ids, w1, b1, w2, b2, wd, wf)


def exchanged(low, high, axis):
    size = lax.axis_size(axis)
    up = [(i, i + 1) for i in range(size - 1)]
    down = [(j, i) for i, j in up]
    return lax.ppermute(high, axis, up), lax.ppermute(low, axis, down)


def image_rows(block_ref, left_ref, right_ref, y):
    return [
        left_ref[8 * y : 8 * y + 8, :].astype(f32),
        block_ref[TW * y : TW * y + TW, :].astype(f32),
        right_ref[8 * y : 8 * y + 8, :].astype(f32),
    ]


def fill(rows, at, block_ref, left_ref, right_ref, first, last):
    for y in range(first, last):
        left, mid, right = image_rows(block_ref, left_ref, right_ref, y)
        base = at + (y - first) * PITCH
        rows[base : base + 8, :] = left
        rows[base + 8 : base + 8 + TW, :] = mid
        rows[base + 8 + TW : base + PITCH, :] = right


def conv_rows(source, at, first, count, main_ref, last, bias, shifted, partial, emit):
    total = (count + 4) * PITCH
    for j in range(5):
        shifted[:total, j * FEAT : (j + 1) * FEAT] = source[
            at + first + j : at + first + j + total, :
        ].astype(bf16)
    span = (count + 1) * PITCH
    parts = 1 if count == 4 else 5
    size = span // parts
    for p in range(parts):
        rows = slice(p * size, (p + 1) * size)
        below = slice(p * size + 2 * PITCH, (p + 1) * size + 2 * PITCH)
        partial[rows, :] = dot_nn(shifted[rows, :], main_ref[: 5 * FEAT, :]) + dot_nn(
            shifted[below, :], main_ref[5 * FEAT :, :]
        )
    for p in range(count // 4):
        base = p * 4 * PITCH
        rows = slice(base, base + 4 * PITCH)
        low = slice(base + PITCH, base + 5 * PITCH)
        end = slice(base + 4 * PITCH, base + 8 * PITCH)
        emit(
            p,
            partial[rows, :FEAT]
            + partial[low, FEAT:]
            + (dot_nn(shifted[end, :], last) + bias),
        )


def hidden_rows(value, first_row):
    flat = iota((4 * PITCH, FEAT), 0)
    col = lax.axis_index("depth") * TW - 2 + flat % PITCH
    row = lax.axis_index("rays") * TH + first_row + flat // PITCH
    inside = (row >= 0) & (row < HEIGHT) & (col >= 0) & (col < WIDE)
    return jnp.where(inside, jnp.maximum(value, 0.0), 0.0)


def inner_kernel(
    block_ref, left_ref, right_ref, main_ref, k_ref, b_ref, out_ref, rows, shifted, partial
):
    fill(rows, 0, block_ref, left_ref, right_ref, 0, TH)
    rows[TH * PITCH :, :] = jnp.zeros((16, FEAT), f32)

    def emit(p, value):
        out_ref[p * 4 * PITCH : (p + 1) * 4 * PITCH, :] = hidden_rows(value, 2 + 4 * p).astype(bf16)

    conv_rows(rows, 0, 4, 12, main_ref, k_ref[4], b_ref[...], shifted, partial, emit)


def outer_kernel(
    block_ref,
    left_ref,
    right_ref,
    above_ref,
    below_ref,
    inner_ref,
    main1_ref,
    k1_ref,
    b1_ref,
    main2_ref,
    k2_ref,
    b2_ref,
    out_ref,
    rows,
    hidden,
    shifted,
    partial,
):
    quad = 4 * PITCH
    rows[:quad, :] = above_ref[...].astype(f32)
    fill(rows, quad, block_ref, left_ref, right_ref, 0, 4)
    rows[2 * quad : 2 * quad + 16, :] = jnp.zeros((16, FEAT), f32)
    second = 2 * quad + 16
    fill(rows, second, block_ref, left_ref, right_ref, TH - 4, TH)
    rows[second + quad : second + 2 * quad, :] = below_ref[...].astype(f32)
    rows[second + 2 * quad :, :] = jnp.zeros((16, FEAT), f32)
    hidden[quad : 4 * quad, :] = inner_ref[...].astype(f32)
    hidden[5 * quad :, :] = jnp.zeros((16, FEAT), f32)
    for n, (at, first_row) in enumerate(((0, -2), (second, TH - 2))):

        def emit(p, value, n=n, first_row=first_row):
            hidden[4 * n * quad : (4 * n + 1) * quad, :] = hidden_rows(value, first_row)

        conv_rows(
            rows, at, 4, 4, main1_ref, k1_ref[4], b1_ref[...], shifted.at[n], partial.at[n], emit
        )

    def finish(p, value):
        value = value.astype(bf16)
        for y in range(4):
            out_ref[p * 4 + y] = value[y * PITCH : y * PITCH + TW, :]

    conv_rows(
        hidden, 0, 0, TH, main2_ref, k2_ref[4], b2_ref[...], shifted.at[2], partial.at[2], finish
    )


def on_device(
    encodings,
    spacing,
    ray_ids,
    live_count,
    pixel_of_ray,
    w_first,
    b_first,
    w_second,
    b_second,
    w_density,
    w_feature,
    kernel_one,
    bias_one,
    kernel_two,
    bias_two,
):
    pixel = pixel_of_ray.reshape(RAYS // LANES, LANES)
    near, far, ray = segments(
        live_count.reshape(1),
        encodings.reshape(SLOTS * SAMPLES, FEAT),
        spacing[0],
        pixel,
        ray_ids.reshape(SLOTS // LANES, LANES),
        w_first,
        b_first,
        w_second,
        b_second,
        w_density,
        w_feature,
    )
    arrived = lax.ppermute(far, "depth", [(i, i ^ 1) for i in range(8)])
    piece = shape_of((PACK, FEAT), bf16)
    pieces = pl.pallas_call(
        pair_kernel,
        in_specs=[HBM] * 2,
        out_specs=[HBM] * 4,
        out_shape=[piece] * 4,
        scratch_shapes=[pltpu.VMEM((4, PACK, FEAT), bf16)] * 3
        + [pltpu.SemaphoreType.DMA((8,)), pltpu.SemaphoreType.DMA((4,))],
        name="pair",
    )(near, arrived)
    got = [
        lax.ppermute(pieces[k], "depth", [(i, (i + 2 * k) % 8) for i in range(8)])
        for k in range(1, 4)
    ]
    taps1, taps2 = kernel_one.reshape(5, 5 * FEAT, FEAT), kernel_two.reshape(5, 5 * FEAT, FEAT)
    main = shape_of((10 * FEAT, 2 * FEAT), bf16)
    info, main1, main2 = pl.pallas_call(
        info_kernel,
        in_specs=[VMEM] * 4,
        out_specs=[VMEM] * 3,
        out_shape=[shape_of((4, 16, LANES), f32), main, main],
        name="info",
    )(pixel, ray, taps1, taps2)
    outgoing = pl.pallas_call(
        merge_kernel,
        in_specs=[VMEM] * 5,
        out_specs=VMEM,
        out_shape=shape_of((32, 40, FEAT), bf16),
        name="merge",
    )(pieces[0], *got, info)
    incoming = lax.all_to_all(outgoing, "rays", split_axis=0, concat_axis=0, tiled=True)
    edge = shape_of((TH * 8, FEAT), bf16)
    block, low_edge, high_edge = pl.pallas_call(
        place_kernel,
        in_specs=[VMEM],
        out_specs=[VMEM] * 3,
        out_shape=[shape_of((TH * TW, FEAT), bf16), edge, edge],
        name="place",
    )(incoming)
    left, right = exchanged(low_edge, high_edge, "depth")
    parts = [left.reshape(TH, 8, FEAT), block.reshape(TH, TW, FEAT), right.reshape(TH, 8, FEAT)]
    first = jnp.concatenate([p[:HALO] for p in parts], axis=1).reshape(HALO * PITCH, FEAT)
    last = jnp.concatenate([p[TH - HALO :] for p in parts], axis=1).reshape(HALO * PITCH, FEAT)
    above, below = exchanged(first, last, "rays")
    inner = pl.pallas_call(
        inner_kernel,
        in_specs=[VMEM] * 6,
        out_specs=VMEM,
        out_shape=shape_of((12 * PITCH, FEAT), bf16),
        scratch_shapes=[
            pltpu.VMEM((TH * PITCH + 16, FEAT), f32),
            pltpu.VMEM((TH * PITCH, 5 * FEAT), bf16),
            pltpu.VMEM((13 * PITCH, 2 * FEAT), f32),
        ],
        name="inner",
    )(block, left, right, main1, taps1, bias_one[None])
    return pl.pallas_call(
        outer_kernel,
        in_specs=[VMEM] * 12,
        out_specs=VMEM,
        out_shape=shape_of((TH, TW, FEAT), bf16),
        scratch_shapes=[
            pltpu.VMEM((16 * PITCH + 32, FEAT), f32),
            pltpu.VMEM((20 * PITCH + 16, FEAT), f32),
            pltpu.VMEM((3, 20 * PITCH, 5 * FEAT), bf16),
            pltpu.VMEM((3, 17 * PITCH, 2 * FEAT), f32),
        ],
        name="outer",
    )(
        block,
        left,
        right,
        above,
        below,
        inner,
        main1,
        taps1,
        bias_one[None],
        main2,
        taps2,
        bias_two[None],
    )


def solution(mesh):
    in_specs = (
        P("depth", "rays", None, None),
        P("depth", None, "rays"),
        P("depth", "rays"),
        P("depth", "rays"),
        P("rays"),
        P("depth", None, None),
        P("depth", None),
        P("depth", None, None),
        P("depth", None),
        P("depth", None),
        P("depth", None, None),
        P(),
        P(),
        P(),
        P(),
    )
    return jax.shard_map(
        on_device, mesh=mesh, in_specs=in_specs, out_specs=P("rays", "depth", None), check_vma=False
    )
```

time: 136 us -> 105 us (0.77)
  the two profiles are of different devices: /device:TPU:41 before, /device:TPU:15 now
where the time goes in v2:
time: 105 us
  Pallas kernels  45.1 us (43%)
  blocking collectives  22.3 us (21%)
  starting transfers between devices  17.8 us (17%)
  waiting for transfers between devices  15.6 us (15%)
  local copies, waits for them, and re-layouts  3.22 us (3%)
    pallas_call x1, Pallas kernels, segments(): pl.pallas_call(segment_kernel, grid_spec=pltpu.PrefetchScalarGridSpec(num...  23.9 us
    all_to_all x1, blocking collectives, on_device(): lax.all_to_all(outgoing, 'rays', split_axis=0, concat_axis=0, tiled=True)  22.3 us
    ppermute x4, starting transfers between devices, exchanged(): return (lax.ppermute(high, axis, up), lax.ppermute(low, axis, down))  12.8 us
    ppermute x3, waiting for transfers between devices, on_device(): lax.ppermute(pieces[k], 'depth', [(i, (i + 2 * k) % 8) for i in range(8)])  7.84 us
    pallas_call x1, Pallas kernels, on_device(): pl.pallas_call(outer_kernel, in_specs=[VMEM] * 12, out_specs=VMEM, out_sh...  5.55 us
    ppermute x4, waiting for transfers between devices, exchanged(): return (lax.ppermute(high, axis, up), lax.ppermute(low, axis, down))  5.27 us
    ppermute x3, starting transfers between devices, on_device(): lax.ppermute(pieces[k], 'depth', [(i, (i + 2 * k) % 8) for i in range(8)])  4.16 us
    pallas_call x1, Pallas kernels, on_device(): pl.pallas_call(info_kernel, in_specs=[VMEM] * 4, out_specs=[VMEM] * 3, ou...  3.73 us
  transfers between devices with their start and end apart: 8, of which 5 were waited for; matrix products, arithmetic and copies ran while one was open for 1% of the time, Pallas kernels for 7%

profile of v2, /device:TPU:15, one launch (start us, length us, event | category | flops | bytes accessed | tf_op | source)
XLA Modules:
  0.0 104.8 jit_solution(11814731833072184190)
XLA Ops:
  0.7 23.9 %segments.1 = (bf16[4,1040,128]{2,1,0:T(8,128)(2,1)}, bf16[4,1040,128]{2,1,0:T(8,128)(2,1)}, s32[64,128]{1,0:T(8,128)}) custom-call(s32[1]{0:T(128)} %bitcast.21.live_smem, bf16[40960,128]{1,0:T(8,128)(2,1)} %bitcast.22, f32[8,5120]{1,0:T(8,128)} %bitcast.30, s32[64,128]{1,0:T(8,128)} %bitcast.31, s32[40,128]{1,0:T(8,128)} %bitcast.35, ...), custom_call_target="tpu_custom_call" | custom-call | tf_op jit(solution)/shard_map/segments/pallas_call | solution.py:420
  24.6 0.8 collective-permute-start
  25.3 2.5 %collective-permute-done.arrived_hbm = bf16[4,1040,128]{2,1,0:T(8,128)(2,1)S(1)} collective-permute-done((bf16[4,1040,128]{2,1,0:T(8,128)(2,1)}, bf16[4,1040,128]{2,1,0:T(8,128)(2,1)S(1)}, u32[]{:S(2)}, u32[]{:S(2)}) %collective-permute-start) | collective-permute-done | bytes 1064992 | tf_op jit(solution)/shard_map/ppermute | solution.py:603
  27.9 1.0 copy-done
  28.8 3.2 %pair.1 = (bf16[1040,128]{1,0:T(8,128)(2,1)}, bf16[1040,128]{1,0:T(8,128)(2,1)}, bf16[1040,128]{1,0:T(8,128)(2,1)}, bf16[1040,128]{1,0:T(8,128)(2,1)}) custom-call(bf16[4,1040,128]{2,1,0:T(8,128)(2,1)} %get-tuple-element.18.mine_hbm, bf16[4,1040,128]{2,1,0:T(8,128)(2,1)} %copy-done), custom_call_target="tpu_custom_call" | custom-call | tf_op jit(solution)/shard_map/pair/pallas_call | solution.py:605
  32.0 1.4 %collective-permute-start.1 = (bf16[1040,128]{1,0:T(8,128)(2,1)}, bf16[1040,128]{1,0:T(8,128)(2,1)S(1)}, u32[]{:S(2)}, u32[]{:S(2)}) collective-permute-start(bf16[1040,128]{1,0:T(8,128)(2,1)} %get-tuple-element.21), channel_id=1, source_target_pairs={{0,64},{32,96},{64,128},{96,160},{128,192},{160,224},{192,0},{224,... | collective-permute-start | bytes 798728 | tf_op jit(solution)/shard_map/ppermute | solution.py:615
  33.4 0.8 collective-permute-start.2
  34.2 2.0 %collective-permute-start.3 = (bf16[1040,128]{1,0:T(8,128)(2,1)}, bf16[1040,128]{1,0:T(8,128)(2,1)S(1)}, u32[]{:S(2)}, u32[]{:S(2)}) collective-permute-start(bf16[1040,128]{1,0:T(8,128)(2,1)} %get-tuple-element.23), channel_id=1, source_target_pairs={{0,192},{32,224},{64,0},{96,32},{128,64},{160,96},{192,128},{224,1... | collective-permute-start | bytes 798728 | tf_op jit(solution)/shard_map/ppermute | solution.py:615
  36.2 3.7 %info.1 = (f32[4,16,128]{2,1,0:T(8,128)}, bf16[1280,256]{1,0:T(8,128)(2,1)}, bf16[1280,256]{1,0:T(8,128)(2,1)}) custom-call(s32[64,128]{1,0:T(8,128)} %bitcast.32, s32[64,128]{1,0:T(8,128)} %get-tuple-element.24.ray_ref, bf16[5,640,128]{2,1,0:T(8,128)(2,1)} %bitcast.23, bf16[5,640,128]{2,1,0:T(8,128)(2,1)} %bitcast.26), custom_call_target="tpu_custom_call" | custom-call | tf_op jit(solution)/shard_map/info/pallas_call | solution.py:620
  39.9 0.0 collective-permute-done.1.p1_ref
  39.9 2.6 %collective-permute-done.2.p2_ref = bf16[1040,128]{1,0:T(8,128)(2,1)S(1)} collective-permute-done((bf16[1040,128]{1,0:T(8,128)(2,1)}, bf16[1040,128]{1,0:T(8,128)(2,1)S(1)}, u32[]{:S(2)}, u32[]{:S(2)}) %collective-permute-start.2) | collective-permute-done | bytes 266272 | tf_op jit(solution)/shard_map/ppermute | solution.py:615
  42.5 5.3 %collective-permute-done.3.p3_ref = bf16[1040,128]{1,0:T(8,128)(2,1)S(1)} collective-permute-done((bf16[1040,128]{1,0:T(8,128)(2,1)}, bf16[1040,128]{1,0:T(8,128)(2,1)S(1)}, u32[]{:S(2)}, u32[]{:S(2)}) %collective-permute-start.3) | collective-permute-done | bytes 266272 | tf_op jit(solution)/shard_map/ppermute | solution.py:615
  47.8 0.0 copy-done.1
  47.8 0.7 copy-done.3
  48.5 2.7 %merge.1 = bf16[32,40,128]{2,1,0:T(8,128)(2,1)} custom-call(bf16[1040,128]{1,0:T(8,128)(2,1)} %get-tuple-element.20.p0_ref, bf16[1040,128]{1,0:T(8,128)(2,1)} %copy-done.1, bf16[1040,128]{1,0:T(8,128)(2,1)} %copy-done.2, bf16[1040,128]{1,0:T(8,128)(2,1)} %copy-done.3, f32[4,16,128]{2,1,0:T(8,128)} %get-tuple-element.25.info_ref), custom_call_target="tpu_custom_call" | custom-call | tf_op jit(solution)/shard_map/merge/pallas_call | solution.py:627
  51.2 22.3 %all_to_all.5.in_ref = bf16[32,40,128]{2,1,0:T(8,128)(2,1)} all-to-all(bf16[32,40,128]{2,1,0:T(8,128)(2,1)} %merge.1), channel_id=1, replica_groups=mesh['depth'=8,'rays'=32] {'rays'}, dimensions={0} | all-to-all | bytes 655360 | tf_op jit(solution)/shard_map/all_to_all | solution.py:634
  73.5 2.4 %place.1 = (bf16[1024,128]{1,0:T(8,128)(2,1)}, bf16[128,128]{1,0:T(8,128)(2,1)}, bf16[128,128]{1,0:T(8,128)(2,1)}) custom-call(bf16[32,40,128]{2,1,0:T(8,128)(2,1)} %all_to_all.5.in_ref), custom_call_target="tpu_custom_call" | custom-call | tf_op jit(solution)/shard_map/place/pallas_call | solution.py:636
  75.9 5.1 %collective-permute-start.4 = (bf16[128,128]{1,0:T(8,128)(2,1)}, bf16[128,128]{1,0:T(8,128)(2,1)S(1)}, u32[]{:S(2)}, u32[]{:S(2)}) collective-permute-start(bf16[128,128]{1,0:T(8,128)(2,1)} %get-tuple-element.27), channel_id=1, source_target_pairs={{0,32},{32,64},{64,96},{96,128},{128,160},{160,192},{192,224},{1,3... | collective-permute-start | bytes 98312 | tf_op jit(solution)/shard_map/ppermute | solution.py:456
  81.0 1.9 %collective-permute-start.5 = (bf16[128,128]{1,0:T(8,128)(2,1)}, bf16[128,128]{1,0:T(8,128)(2,1)S(1)}, u32[]{:S(2)}, u32[]{:S(2)}) collective-permute-start(bf16[128,128]{1,0:T(8,128)(2,1)} %get-tuple-element.28), channel_id=1, source_target_pairs={{32,0},{64,32},{96,64},{128,96},{160,128},{192,160},{224,192},{33,... | collective-permute-start | bytes 98312 | tf_op jit(solution)/shard_map/ppermute | solution.py:456
  83.0 0.9 fusion
  83.8 0.0 collective-permute-done.4.left_ref
  83.9 2.6 %collective-permute-done.5.right_ref = bf16[128,128]{1,0:T(8,128)(2,1)S(1)} collective-permute-done((bf16[128,128]{1,0:T(8,128)(2,1)}, bf16[128,128]{1,0:T(8,128)(2,1)S(1)}, u32[]{:S(2)}, u32[]{:S(2)}) %collective-permute-start.5) | collective-permute-done | bytes 32800 | tf_op jit(solution)/shard_map/ppermute | solution.py:456
  86.5 3.9 %collective-permute-start.6 = (bf16[320,128]{1,0:T(8,128)(2,1)S(1)}, bf16[320,128]{1,0:T(8,128)(2,1)S(1)}, u32[]{:S(2)}, u32[]{:S(2)}) collective-permute-start(bf16[320,128]{1,0:T(8,128)(2,1)S(1)} %bitcast.33), channel_id=1, source_target_pairs={{0,1},{1,2},{2,3},{3,4},{4,5},{5,6},{6,7},{7,8},{8,9},{9,10},{10,1... | collective-permute-start | bytes 245768 | tf_op jit(solution)/shard_map/ppermute | solution.py:456
  90.4 1.9 %collective-permute-start.7 = (bf16[320,128]{1,0:T(8,128)(2,1)S(1)}, bf16[320,128]{1,0:T(8,128)(2,1)S(1)}, u32[]{:S(2)}, u32[]{:S(2)}) collective-permute-start(bf16[320,128]{1,0:T(8,128)(2,1)S(1)} %bitcast.34), channel_id=1, source_target_pairs={{1,0},{2,1},{3,2},{4,3},{5,4},{6,5},{7,6},{8,7},{9,8},{10,9},{11,1... | collective-permute-start | bytes 245768 | tf_op jit(solution)/shard_map/ppermute | solution.py:456
  92.3 0.0 copy-done.4
  92.3 0.0 copy-done.5
  92.4 3.6 %inner.1.inner_ref = bf16[960,128]{1,0:T(8,128)(2,1)} custom-call(bf16[1024,128]{1,0:T(8,128)(2,1)} %get-tuple-element.26.block_ref, bf16[128,128]{1,0:T(8,128)(2,1)} %copy-done.4, bf16[128,128]{1,0:T(8,128)(2,1)} %copy-done.5, bf16[1280,256]{1,0:T(8,128)(2,1)} %get-tuple-element.29.main_ref.main1_ref, bf16[5,640,128]{2,1,0:T(8,128)(2,1)} %bitcast.24, ...), custom_call_target="tpu_custom_call" | custom-call | tf_op jit(solution)/shard_map/inner/pallas_call | solution.py:648
  96.0 0.0 collective-permute-done.6.above_ref
  96.0 2.7 %collective-permute-done.7.below_ref = bf16[320,128]{1,0:T(8,128)(2,1)S(1)} collective-permute-done((bf16[320,128]{1,0:T(8,128)(2,1)S(1)}, bf16[320,128]{1,0:T(8,128)(2,1)S(1)}, u32[]{:S(2)}, u32[]{:S(2)}) %collective-permute-start.7) | collective-permute-done | bytes 81952 | tf_op jit(solution)/shard_map/ppermute | solution.py:456
  98.6 0.0 copy-done.6
  98.6 0.6 copy-done.7
  99.3 5.5 %outer.1 = bf16[16,64,128]{2,1,0:T(8,128)(2,1)} custom-call(bf16[1024,128]{1,0:T(8,128)(2,1)} %get-tuple-element.26.block_ref, bf16[128,128]{1,0:T(8,128)(2,1)} %copy-done.4, bf16[128,128]{1,0:T(8,128)(2,1)} %copy-done.5, bf16[320,128]{1,0:T(8,128)(2,1)} %copy-done.6, bf16[320,128]{1,0:T(8,128)(2,1)} %copy-done.7, bf16[960,128]{1,0:T(8,128)(2,1)} %inner.1.inner_ref, ...), custom_call_target="tpu_custom_call" | custom-call | tf_op jit(solution)/shard_map/outer/pallas_call | solution.py:660
  (13 shorter events, 0.0 us)
Async XLA Ops:
  24.6 3.3 %collective-permute-start = (bf16[4,1040,128]{2,1,0:T(8,128)(2,1)}, bf16[4,1040,128]{2,1,0:T(8,128)(2,1)S(1)}, u32[]{:S(2)}, u32[]{:S(2)}) collective-permute-start(bf16[4,1040,128]{2,1,0:T(8,128)(2,1)} %get-tuple-element.19), channel_id=1, source_target_pairs={{0,32},{32,0},{64,96},{96,64},{128,160},{160,128},{192,224},{224,1... | collective-permute-start | bytes 3194888 | tf_op jit(solution)/shard_map/ppermute | solution.py:603
  27.9 1.0 copy-start
  32.0 7.9 %collective-permute-start.1 = (bf16[1040,128]{1,0:T(8,128)(2,1)}, bf16[1040,128]{1,0:T(8,128)(2,1)S(1)}, u32[]{:S(2)}, u32[]{:S(2)}) collective-permute-start(bf16[1040,128]{1,0:T(8,128)(2,1)} %get-tuple-element.21), channel_id=1, source_target_pairs={{0,64},{32,96},{64,128},{96,160},{128,192},{160,224},{192,0},{224,... | collective-permute-start | bytes 798728 | tf_op jit(solution)/shard_map/ppermute | solution.py:615
  33.4 9.1 %collective-permute-start.2 = (bf16[1040,128]{1,0:T(8,128)(2,1)}, bf16[1040,128]{1,0:T(8,128)(2,1)S(1)}, u32[]{:S(2)}, u32[]{:S(2)}) collective-permute-start(bf16[1040,128]{1,0:T(8,128)(2,1)} %get-tuple-element.22), channel_id=1, source_target_pairs={{0,128},{32,160},{64,192},{96,224},{128,0},{160,32},{192,64},{224,... | collective-permute-start | bytes 798728 | tf_op jit(solution)/shard_map/ppermute | solution.py:615
  34.2 13.5 %collective-permute-start.3 = (bf16[1040,128]{1,0:T(8,128)(2,1)}, bf16[1040,128]{1,0:T(8,128)(2,1)S(1)}, u32[]{:S(2)}, u32[]{:S(2)}) collective-permute-start(bf16[1040,128]{1,0:T(8,128)(2,1)} %get-tuple-element.23), channel_id=1, source_target_pairs={{0,192},{32,224},{64,0},{96,32},{128,64},{160,96},{192,128},{224,1... | collective-permute-start | bytes 798728 | tf_op jit(solution)/shard_map/ppermute | solution.py:615
  39.9 7.8 %copy-start.1 = (bf16[1040,128]{1,0:T(8,128)(2,1)}, bf16[1040,128]{1,0:T(8,128)(2,1)S(1)}, u32[]{:S(2)}) copy-start(bf16[1040,128]{1,0:T(8,128)(2,1)S(1)} %collective-permute-done.1.p1_ref) | copy-start | bytes 798724
  42.5 5.3 %copy-start.2 = (bf16[1040,128]{1,0:T(8,128)(2,1)}, bf16[1040,128]{1,0:T(8,128)(2,1)S(1)}, u32[]{:S(2)}) copy-start(bf16[1040,128]{1,0:T(8,128)(2,1)S(1)} %collective-permute-done.2.p2_ref) | copy-start | bytes 798724
  47.8 0.7 copy-start.3
  75.9 7.9 %collective-permute-start.4 = (bf16[128,128]{1,0:T(8,128)(2,1)}, bf16[128,128]{1,0:T(8,128)(2,1)S(1)}, u32[]{:S(2)}, u32[]{:S(2)}) collective-permute-start(bf16[128,128]{1,0:T(8,128)(2,1)} %get-tuple-element.27), channel_id=1, source_target_pairs={{0,32},{32,64},{64,96},{96,128},{128,160},{160,192},{192,224},{1,3... | collective-permute-start | bytes 98312 | tf_op jit(solution)/shard_map/ppermute | solution.py:456
  81.0 5.4 %collective-permute-start.5 = (bf16[128,128]{1,0:T(8,128)(2,1)}, bf16[128,128]{1,0:T(8,128)(2,1)S(1)}, u32[]{:S(2)}, u32[]{:S(2)}) collective-permute-start(bf16[128,128]{1,0:T(8,128)(2,1)} %get-tuple-element.28), channel_id=1, source_target_pairs={{32,0},{64,32},{96,64},{128,96},{160,128},{192,160},{224,192},{33,... | collective-permute-start | bytes 98312 | tf_op jit(solution)/shard_map/ppermute | solution.py:456
  83.9 8.5 %copy-start.4 = (bf16[128,128]{1,0:T(8,128)(2,1)}, bf16[128,128]{1,0:T(8,128)(2,1)S(1)}, u32[]{:S(2)}) copy-start(bf16[128,128]{1,0:T(8,128)(2,1)S(1)} %collective-permute-done.4.left_ref) | copy-start | bytes 98308
  86.5 5.9 %copy-start.5 = (bf16[128,128]{1,0:T(8,128)(2,1)}, bf16[128,128]{1,0:T(8,128)(2,1)S(1)}, u32[]{:S(2)}) copy-start(bf16[128,128]{1,0:T(8,128)(2,1)S(1)} %collective-permute-done.5.right_ref) | copy-start | bytes 98308
  86.5 9.5 %collective-permute-start.6 = (bf16[320,128]{1,0:T(8,128)(2,1)S(1)}, bf16[320,128]{1,0:T(8,128)(2,1)S(1)}, u32[]{:S(2)}, u32[]{:S(2)}) collective-permute-start(bf16[320,128]{1,0:T(8,128)(2,1)S(1)} %bitcast.33), channel_id=1, source_target_pairs={{0,1},{1,2},{2,3},{3,4},{4,5},{5,6},{6,7},{7,8},{8,9},{9,10},{10,1... | collective-permute-start | bytes 245768 | tf_op jit(solution)/shard_map/ppermute | solution.py:456
  90.4 8.2 %collective-permute-start.7 = (bf16[320,128]{1,0:T(8,128)(2,1)S(1)}, bf16[320,128]{1,0:T(8,128)(2,1)S(1)}, u32[]{:S(2)}, u32[]{:S(2)}) collective-permute-start(bf16[320,128]{1,0:T(8,128)(2,1)S(1)} %bitcast.34), channel_id=1, source_target_pairs={{1,0},{2,1},{3,2},{4,3},{5,4},{6,5},{7,6},{8,7},{9,8},{10,9},{11,1... | collective-permute-start | bytes 245768 | tf_op jit(solution)/shard_map/ppermute | solution.py:456
  96.0 2.7 %copy-start.6 = (bf16[320,128]{1,0:T(8,128)(2,1)}, bf16[320,128]{1,0:T(8,128)(2,1)S(1)}, u32[]{:S(2)}) copy-start(bf16[320,128]{1,0:T(8,128)(2,1)S(1)} %collective-permute-done.6.above_ref) | copy-start | bytes 245764
  98.6 0.6 copy-start.7

commit v3 on v2

--- a/solution.py
+++ b/solution.py
@@ -18,7 +18,7 @@
 LANES = 128
 HALO = 4
 PITCH = TW + 16
-PAIR_ORDER = (2, 1, 3, 0)
+SMALL = pltpu.CompilerParams(vmem_limit_bytes=24 << 20)
 PIECE = 1024
 PACK = PIECE + 16
 SUPER = 256
@@ -141,8 +141,8 @@
     b2_ref,
     wd_ref,
     wf_ref,
-    near_hbm,
-    far_hbm,
+    near_ref,
+    far_ref,
     ray_ref,
     spread,
     hidden,
@@ -157,9 +157,7 @@
     table_ref,
     pos_ref,
     pos_smem,
-    staged,
     pos_sem,
-    out_sems,
 ):
     step = pl.program_id(0)
     to_smem = pltpu.make_async_copy(pos_ref, pos_smem, pos_sem)
@@ -287,20 +285,15 @@
                 table_ref[...] = depth_table(2 * t + 1, table)
 
         table = table_ref[...]
-        stores = []
         for n in range(8):
             k, g = 1 - n // 4, n % 4
             at = (4 * k + g) * PIECE
-            staged[n, :PIECE, :] = spread[at : at + PIECE, :].astype(bf16)
+            out = (near_ref, far_ref)[k]
+            out[g, :PIECE, :] = spread[at : at + PIECE, :].astype(bf16)
             rows = (4 * k + g) * 8
-            staged[n, PIECE:, :] = jnp.concatenate(
+            out[g, PIECE:, :] = jnp.concatenate(
                 [table[rows : rows + 8], table[64 + rows : 72 + rows]], axis=0
             ).astype(bf16)
-            out = (near_hbm, far_hbm)[k].at[g]
-            stores.append(pltpu.make_async_copy(staged.at[n], out, out_sems.at[n]))
-            stores[-1].start()
-        for store in stores:
-            store.wait()
 
 
 def read_depth(ref):
@@ -312,25 +305,11 @@
     return ref[i * LANES : (i + 1) * LANES, :].astype(f32) * factors[:, i : i + 1]
 
 
-def pair_kernel(mine_hbm, arrived_hbm, o0, o1, o2, o3, mine, arrived, done, in_sems, out_sems):
+def pair_kernel(mine, arrived, o0, o1, o2, o3):
     my_core, _, _ = coordinates()
-    loads = [
-        (
-            pltpu.make_async_copy(mine_hbm.at[g], mine.at[g], in_sems.at[2 * g]),
-            pltpu.make_async_copy(arrived_hbm.at[g], arrived.at[g], in_sems.at[2 * g + 1]),
-        )
-        for g in PAIR_ORDER
-    ]
-    for two in loads:
-        for load in two:
-            load.start()
-
     def combine(front_all, back_all):
-        stores = []
-        for g, two in zip(PAIR_ORDER, loads):
-            for load in two:
-                load.wait()
-            front, back, out = front_all.at[g], back_all.at[g], done.at[g]
+        for g in range(4):
+            front, back, out = front_all.at[g], back_all.at[g], (o0, o1, o2, o3)[g]
             d_front, d_back = read_depth(front), read_depth(back)
             fade = jnp.exp(-d_front).T
             for i in range(8):
@@ -339,11 +318,6 @@
             both = d_front + d_back
             coarse = both.astype(bf16).astype(f32)
             out[PIECE:, :] = jnp.concatenate([coarse, both - coarse], axis=0).astype(bf16)
-            store = pltpu.make_async_copy(out, (o0, o1, o2, o3)[g], out_sems.at[g])
-            store.start()
-            stores.append(store)
-        for store in stores:
-            store.wait()
 
     @pl.when(my_core == 0)
     def _():
@@ -402,6 +376,14 @@
     ).astype(bf16)
 
 
+def on_chip(array):
+    return pltpu.with_memory_space_constraint(array, pltpu.VMEM)
+
+
+def off_chip(array):
+    return pltpu.with_memory_space_constraint(array, pltpu.HBM)
+
+
 def whole(shape):
     return pl.BlockSpec(shape, lambda *_: (0,) * len(shape))
 
@@ -411,12 +393,11 @@
 
 
 VMEM = pl.BlockSpec(memory_space=pltpu.VMEM)
-HBM = pl.BlockSpec(memory_space=pltpu.HBM)
 
 
 def segments(live, enc, gaps, pixel, ids, w1, b1, w2, b2, wd, wf):
     rows = 2 * SUPER * SAMPLES
-    out = shape_of((4, PACK, FEAT), bf16)
+    out = pltpu.VMEM((4, PACK, FEAT), bf16)
     return pl.pallas_call(
         segment_kernel,
         grid_spec=pltpu.PrefetchScalarGridSpec(
@@ -424,7 +405,7 @@
             grid=(SLOTS * SAMPLES // rows,),
             in_specs=[pl.BlockSpec((rows, FEAT), lambda i, *_: (i, 0))]
             + [whole(a.shape) for a in (gaps, pixel, ids, w1, b1, w2, b2, wd, wf)],
-            out_specs=[HBM, HBM, whole(pixel.shape)],
+            out_specs=[VMEM, VMEM, whole(pixel.shape)],
             scratch_shapes=[
                 pltpu.VMEM((RAYS, FEAT), f32),
                 pltpu.VMEM((SLOTS * SAMPLES // 2, 2 * FEAT), bf16),
@@ -439,14 +420,13 @@
                 pltpu.VMEM((2 * RAYS // LANES, LANES), f32),
                 pltpu.VMEM((SLOTS // LANES, LANES), i32),
                 pltpu.SMEM((SLOTS // LANES, LANES), i32),
-                pltpu.VMEM((8, PACK, FEAT), bf16),
                 pltpu.SemaphoreType.DMA,
-                pltpu.SemaphoreType.DMA((8,)),
             ],
         ),
         out_shape=[out, out, shape_of(pixel.shape, i32)],
+        compiler_params=pltpu.CompilerParams(vmem_limit_bytes=40 << 20),
         name="segments",
-    )(live, enc, gaps, pixel, ids, w1, b1, w2, b2, wd, wf)
+    )(live, *[off_chip(a) for a in (enc, gaps, pixel, ids, w1, b1, w2, b2, wd, wf)])
 
 
 def exchanged(low, high, axis):
@@ -601,36 +581,37 @@
         w_feature,
     )
     arrived = lax.ppermute(far, "depth", [(i, i ^ 1) for i in range(8)])
-    piece = shape_of((PACK, FEAT), bf16)
+    piece = pltpu.VMEM((PACK, FEAT), bf16)
     pieces = pl.pallas_call(
         pair_kernel,
-        in_specs=[HBM] * 2,
-        out_specs=[HBM] * 4,
+        in_specs=[VMEM] * 2,
+        out_specs=[VMEM] * 4,
         out_shape=[piece] * 4,
-        scratch_shapes=[pltpu.VMEM((4, PACK, FEAT), bf16)] * 3
-        + [pltpu.SemaphoreType.DMA((8,)), pltpu.SemaphoreType.DMA((4,))],
+        compiler_params=SMALL,
         name="pair",
-    )(near, arrived)
+    )(near, on_chip(arrived))
     got = [
         lax.ppermute(pieces[k], "depth", [(i, (i + 2 * k) % 8) for i in range(8)])
         for k in range(1, 4)
     ]
     taps1, taps2 = kernel_one.reshape(5, 5 * FEAT, FEAT), kernel_two.reshape(5, 5 * FEAT, FEAT)
-    main = shape_of((10 * FEAT, 2 * FEAT), bf16)
+    main = pltpu.VMEM((10 * FEAT, 2 * FEAT), bf16)
     info, main1, main2 = pl.pallas_call(
         info_kernel,
         in_specs=[VMEM] * 4,
         out_specs=[VMEM] * 3,
-        out_shape=[shape_of((4, 16, LANES), f32), main, main],
+        out_shape=[pltpu.VMEM((4, 16, LANES), f32), main, main],
+        compiler_params=SMALL,
         name="info",
     )(pixel, ray, taps1, taps2)
     outgoing = pl.pallas_call(
         merge_kernel,
         in_specs=[VMEM] * 5,
         out_specs=VMEM,
-        out_shape=shape_of((32, 40, FEAT), bf16),
+        out_shape=pltpu.VMEM((32, 40, FEAT), bf16),
+        compiler_params=SMALL,
         name="merge",
-    )(pieces[0], *got, info)
+    )(pieces[0], *[on_chip(g) for g in got], info)
     incoming = lax.all_to_all(outgoing, "rays", split_axis=0, concat_axis=0, tiled=True)
     edge = shape_of((TH * 8, FEAT), bf16)
     block, low_edge, high_edge = pl.pallas_call(
@@ -638,23 +619,27 @@
         in_specs=[VMEM],
         out_specs=[VMEM] * 3,
         out_shape=[shape_of((TH * TW, FEAT), bf16), edge, edge],
+        compiler_params=SMALL,
         name="place",
-    )(incoming)
+    )(on_chip(incoming))
     left, right = exchanged(low_edge, high_edge, "depth")
     parts = [left.reshape(TH, 8, FEAT), block.reshape(TH, TW, FEAT), right.reshape(TH, 8, FEAT)]
     first = jnp.concatenate([p[:HALO] for p in parts], axis=1).reshape(HALO * PITCH, FEAT)
     last = jnp.concatenate([p[TH - HALO :] for p in parts], axis=1).reshape(HALO * PITCH, FEAT)
     above, below = exchanged(first, last, "rays")
+    above, below = on_chip(above), on_chip(below)
+    left, right = on_chip(left), on_chip(right)
     inner = pl.pallas_call(
         inner_kernel,
         in_specs=[VMEM] * 6,
         out_specs=VMEM,
-        out_shape=shape_of((12 * PITCH, FEAT), bf16),
+        out_shape=pltpu.VMEM((12 * PITCH, FEAT), bf16),
         scratch_shapes=[
             pltpu.VMEM((TH * PITCH + 16, FEAT), f32),
             pltpu.VMEM((TH * PITCH, 5 * FEAT), bf16),
             pltpu.VMEM((13 * PITCH, 2 * FEAT), f32),
         ],
+        compiler_params=SMALL,
         name="inner",
     )(block, left, right, main1, taps1, bias_one[None])
     return pl.pallas_call(
@@ -668,6 +653,7 @@
             pltpu.VMEM((3, 20 * PITCH, 5 * FEAT), bf16),
             pltpu.VMEM((3, 17 * PITCH, 2 * FEAT), f32),
         ],
+        compiler_params=SMALL,
         name="outer",
     )(
         block,

time: 105 us -> 92.5 us (0.88)
  Pallas kernels: 45.1 us -> 30.9 us
  waiting for transfers between devices: 15.6 us -> 20.3 us
  local copies, waits for them, and re-layouts: 3.22 us -> 0.04 us
    ppermute x4, waiting for transfers between devices: 5.27 us -> 8.13 us  [exchanged(): return (lax.ppermute(high, axis, up), lax.ppermute(low, axis, down))]
    pallas_call x1, Pallas kernels: 3.2 us -> 0.79 us  [on_device(): pl.pallas_call(pair_kernel, in_specs=[VMEM] * 2, out_specs=[VMEM] * 4, ou...]
    unnamed x16 -> x10, local copies, waits for them, and re-layouts: 2.33 us -> 0.02 us
    pallas_call x1, Pallas kernels: 3.73 us -> 1.47 us  [on_device(): pl.pallas_call(info_kernel, in_specs=[VMEM] * 4, out_specs=[VMEM] * 3, ou...]
    pallas_call x1, Pallas kernels: 3.61 us -> 1.51 us  [on_device(): pl.pallas_call(inner_kernel, in_specs=[VMEM] * 6, out_specs=VMEM, out_sha...]
    ppermute x3, waiting for transfers between devices: 7.84 us -> 9.88 us  [on_device(): lax.ppermute(pieces[k], 'depth', [(i, (i + 2 * k) % 8) for i in range(8)])]
    pallas_call x1, Pallas kernels: 5.55 us -> 3.56 us  [on_device(): pl.pallas_call(outer_kernel, in_specs=[VMEM] * 12, out_specs=VMEM, out_sh...]
    pallas_call x1, Pallas kernels: 2.69 us -> 0.78 us  [on_device(): pl.pallas_call(merge_kernel, in_specs=[VMEM] * 5, out_specs=VMEM, out_sha...]
  transfers between devices with their start and end apart: 8 -> 8, of which waited for: 5 -> 6; matrix products, arithmetic and copies ran while one was open for 1% -> 0% of each run, Pallas kernels for 7% -> 3%
where the time goes in v3:
time: 92.5 us; the launch traced here: 92.1 us
  Pallas kernels  30.9 us (33%)
  blocking collectives  22 us (24%)
  waiting for transfers between devices  20.3 us (22%)
  starting transfers between devices  18 us (19%)
    pallas_call x1, Pallas kernels, segments(): pl.pallas_call(segment_kernel, grid_spec=pltpu.PrefetchScalarGridSpec(num...  22.1 us
    all_to_all x1, blocking collectives, on_device(): lax.all_to_all(outgoing, 'rays', split_axis=0, concat_axis=0, tiled=True)  22 us
    ppermute x4, starting transfers between devices, exchanged(): return (lax.ppermute(high, axis, up), lax.ppermute(low, axis, down))  12.9 us
    ppermute x3, waiting for transfers between devices, on_device(): lax.ppermute(pieces[k], 'depth', [(i, (i + 2 * k) % 8) for i in range(8)])  9.88 us
    ppermute x4, waiting for transfers between devices, exchanged(): return (lax.ppermute(high, axis, up), lax.ppermute(low, axis, down))  8.13 us
    ppermute x3, starting transfers between devices, on_device(): lax.ppermute(pieces[k], 'depth', [(i, (i + 2 * k) % 8) for i in range(8)])  4.35 us
    pallas_call x1, Pallas kernels, on_device(): pl.pallas_call(outer_kernel, in_specs=[VMEM] * 12, out_specs=VMEM, out_sh...  3.56 us
    ppermute x1, waiting for transfers between devices, on_device(): arrived = lax.ppermute(far, 'depth', [(i, i ^ 1) for i in range(8)])  2.31 us
  transfers between devices with their start and end apart: 8, of which 6 were waited for; matrix products, arithmetic and copies ran while one was open for 0% of the time, Pallas kernels for 3%

profile of v3, /device:TPU:15, one launch (start us, length us, event | category | flops | bytes accessed | tf_op | source)
XLA Modules:
  0.0 92.1 jit_solution(3367903655708412114)
XLA Ops:
  0.7 22.1 %segments.1 = (bf16[4,1040,128]{2,1,0:T(8,128)(2,1)S(1)}, bf16[4,1040,128]{2,1,0:T(8,128)(2,1)S(1)}, s32[64,128]{1,0:T(8,128)S(1)}) custom-call(s32[1]{0:T(128)} %bitcast.21.live_smem, bf16[40960,128]{1,0:T(8,128)(2,1)} %bitcast.32, f32[8,5120]{1,0:T(8,128)} %bitcast.35, s32[64,128]{1,0:T(8,128)} %bitcast.27, s32[40,128]{1,0:T(8,128)} %bitcast.38, ...), custom_call_target="tpu_custom_call" | custom-call | tf_op jit(solution)/shard_map/segments/pallas_call | solution.py:401
  22.8 0.8 collective-permute-start
  23.5 2.3 %collective-permute-done.arrived = bf16[4,1040,128]{2,1,0:T(8,128)(2,1)S(1)} collective-permute-done((bf16[4,1040,128]{2,1,0:T(8,128)(2,1)S(1)}, bf16[4,1040,128]{2,1,0:T(8,128)(2,1)S(1)}, u32[]{:S(2)}, u32[]{:S(2)}) %collective-permute-start) | collective-permute-done | bytes 1064992 | tf_op jit(solution)/shard_map/ppermute | solution.py:583
  25.8 0.0 copy-start
  25.8 0.8 pair.1
  26.6 1.6 %collective-permute-start.1 = (bf16[1040,128]{1,0:T(8,128)(2,1)S(1)}, bf16[1040,128]{1,0:T(8,128)(2,1)S(1)}, u32[]{:S(2)}, u32[]{:S(2)}) collective-permute-start(bf16[1040,128]{1,0:T(8,128)(2,1)S(1)} %get-tuple-element.21), channel_id=1, source_target_pairs={{0,64},{32,96},{64,128},{96,160},{128,192},{160,224},{192,0},{224,... | collective-permute-start | bytes 798728 | tf_op jit(solution)/shard_map/ppermute | solution.py:594
  28.2 0.8 collective-permute-start.2
  29.0 2.0 %collective-permute-start.3 = (bf16[1040,128]{1,0:T(8,128)(2,1)S(1)}, bf16[1040,128]{1,0:T(8,128)(2,1)S(1)}, u32[]{:S(2)}, u32[]{:S(2)}) collective-permute-start(bf16[1040,128]{1,0:T(8,128)(2,1)S(1)} %get-tuple-element.23), channel_id=1, source_target_pairs={{0,192},{32,224},{64,0},{96,32},{128,64},{160,96},{192,128},{224,1... | collective-permute-start | bytes 798728 | tf_op jit(solution)/shard_map/ppermute | solution.py:594
  31.0 0.0 copy-done
  31.0 0.0 copy-done.1
  31.0 0.0 copy-done.2
  31.0 1.5 %info.1 = (f32[4,16,128]{2,1,0:T(8,128)S(1)}, bf16[1280,256]{1,0:T(8,128)(2,1)S(1)}, bf16[1280,256]{1,0:T(8,128)(2,1)S(1)}) custom-call(s32[64,128]{1,0:T(8,128)S(1)} %bitcast.28, s32[64,128]{1,0:T(8,128)S(1)} %get-tuple-element.24.ray_ref, bf16[5,640,128]{2,1,0:T(8,128)(2,1)S(1)} %bitcast.22, bf16[5,640,128]{2,1,0:T(8,128)(2,1)S(1)} %bitcast.25), custom_call_target="tpu_custom_call" | custom-call | tf_op jit(solution)/shard_map/info/pallas_call | solution.py:599
  32.5 2.0 %collective-permute-done.1.p1_ref = bf16[1040,128]{1,0:T(8,128)(2,1)S(1)} collective-permute-done((bf16[1040,128]{1,0:T(8,128)(2,1)S(1)}, bf16[1040,128]{1,0:T(8,128)(2,1)S(1)}, u32[]{:S(2)}, u32[]{:S(2)}) %collective-permute-start.1) | collective-permute-done | bytes 266272 | tf_op jit(solution)/shard_map/ppermute | solution.py:594
  34.5 2.6 %collective-permute-done.2.p2_ref = bf16[1040,128]{1,0:T(8,128)(2,1)S(1)} collective-permute-done((bf16[1040,128]{1,0:T(8,128)(2,1)S(1)}, bf16[1040,128]{1,0:T(8,128)(2,1)S(1)}, u32[]{:S(2)}, u32[]{:S(2)}) %collective-permute-start.2) | collective-permute-done | bytes 266272 | tf_op jit(solution)/shard_map/ppermute | solution.py:594
  37.1 5.3 %collective-permute-done.3.p3_ref = bf16[1040,128]{1,0:T(8,128)(2,1)S(1)} collective-permute-done((bf16[1040,128]{1,0:T(8,128)(2,1)S(1)}, bf16[1040,128]{1,0:T(8,128)(2,1)S(1)}, u32[]{:S(2)}, u32[]{:S(2)}) %collective-permute-start.3) | collective-permute-done | bytes 266272 | tf_op jit(solution)/shard_map/ppermute | solution.py:594
  42.3 0.8 merge.1
  43.1 0.0 copy-start.3
  43.1 22.0 %all_to_all.5.in_ref = bf16[32,40,128]{2,1,0:T(8,128)(2,1)S(1)} all-to-all(bf16[32,40,128]{2,1,0:T(8,128)(2,1)S(1)} %merge.1), channel_id=1, replica_groups=mesh['depth'=8,'rays'=32] {'rays'}, dimensions={0} | all-to-all | bytes 655360 | tf_op jit(solution)/shard_map/all_to_all | solution.py:615
  65.2 0.7 place.1
  65.9 5.1 %collective-permute-start.4 = (bf16[128,128]{1,0:T(8,128)(2,1)S(1)}, bf16[128,128]{1,0:T(8,128)(2,1)S(1)}, u32[]{:S(2)}, u32[]{:S(2)}) collective-permute-start(bf16[128,128]{1,0:T(8,128)(2,1)S(1)} %get-tuple-element.27), channel_id=1, source_target_pairs={{0,32},{32,64},{64,96},{96,128},{128,160},{160,192},{192,224},{1,3... | collective-permute-start | bytes 98312 | tf_op jit(solution)/shard_map/ppermute | solution.py:436
  71.0 1.9 %collective-permute-start.5 = (bf16[128,128]{1,0:T(8,128)(2,1)S(1)}, bf16[128,128]{1,0:T(8,128)(2,1)S(1)}, u32[]{:S(2)}, u32[]{:S(2)}) collective-permute-start(bf16[128,128]{1,0:T(8,128)(2,1)S(1)} %get-tuple-element.28), channel_id=1, source_target_pairs={{32,0},{64,32},{96,64},{128,96},{160,128},{192,160},{224,192},{33,... | collective-permute-start | bytes 98312 | tf_op jit(solution)/shard_map/ppermute | solution.py:436
  73.0 0.0 collective-permute-done.4.left_ref
  73.0 3.3 %collective-permute-done.5.right_ref = bf16[128,128]{1,0:T(8,128)(2,1)S(1)} collective-permute-done((bf16[128,128]{1,0:T(8,128)(2,1)S(1)}, bf16[128,128]{1,0:T(8,128)(2,1)S(1)}, u32[]{:S(2)}, u32[]{:S(2)}) %collective-permute-start.5) | collective-permute-done | bytes 32800 | tf_op jit(solution)/shard_map/ppermute | solution.py:436
  76.3 3.9 %collective-permute-start.6 = (bf16[320,128]{1,0:T(8,128)(2,1)S(1)}, bf16[320,128]{1,0:T(8,128)(2,1)S(1)}, u32[]{:S(2)}, u32[]{:S(2)}) collective-permute-start(bf16[320,128]{1,0:T(8,128)(2,1)S(1)} %bitcast.36), channel_id=1, source_target_pairs={{0,1},{1,2},{2,3},{3,4},{4,5},{5,6},{6,7},{7,8},{8,9},{9,10},{10,1... | collective-permute-start | bytes 245768 | tf_op jit(solution)/shard_map/ppermute | solution.py:436
  80.2 0.0 copy-start.4
  80.2 1.9 %collective-permute-start.7 = (bf16[320,128]{1,0:T(8,128)(2,1)S(1)}, bf16[320,128]{1,0:T(8,128)(2,1)S(1)}, u32[]{:S(2)}, u32[]{:S(2)}) collective-permute-start(bf16[320,128]{1,0:T(8,128)(2,1)S(1)} %bitcast.37), channel_id=1, source_target_pairs={{1,0},{2,1},{3,2},{4,3},{5,4},{6,5},{7,6},{8,7},{9,8},{10,9},{11,1... | collective-permute-start | bytes 245768 | tf_op jit(solution)/shard_map/ppermute | solution.py:436
  82.1 0.0 copy-done.3
  82.1 1.5 %inner.1.inner_ref = bf16[960,128]{1,0:T(8,128)(2,1)S(1)} custom-call(bf16[1024,128]{1,0:T(8,128)(2,1)S(1)} %get-tuple-element.26.block_ref, bf16[128,128]{1,0:T(8,128)(2,1)S(1)} %collective-permute-done.4.left_ref, bf16[128,128]{1,0:T(8,128)(2,1)S(1)} %collective-permute-done.5.right_ref, bf16[1280,256]{1,0:T(8,128)(2,1)S(1)} %get-tuple-element.29.main_ref.main1_ref, ...), custom_call_target="tpu_custom_call" | custom-call | tf_op jit(solution)/shard_map/inner/pallas_call | solution.py:632
  83.7 0.0 collective-permute-done.6.above_ref
  83.7 4.9 %collective-permute-done.7.below_ref = bf16[320,128]{1,0:T(8,128)(2,1)S(1)} collective-permute-done((bf16[320,128]{1,0:T(8,128)(2,1)S(1)}, bf16[320,128]{1,0:T(8,128)(2,1)S(1)}, u32[]{:S(2)}, u32[]{:S(2)}) %collective-permute-start.7) | collective-permute-done | bytes 81952 | tf_op jit(solution)/shard_map/ppermute | solution.py:436
  88.5 0.0 copy-done.4
  88.5 3.6 %outer.1 = bf16[16,64,128]{2,1,0:T(8,128)(2,1)} custom-call(bf16[1024,128]{1,0:T(8,128)(2,1)S(1)} %get-tuple-element.26.block_ref, bf16[128,128]{1,0:T(8,128)(2,1)S(1)} %collective-permute-done.4.left_ref, bf16[128,128]{1,0:T(8,128)(2,1)S(1)} %collective-permute-done.5.right_ref, bf16[320,128]{1,0:T(8,128)(2,1)S(1)} %collective-permute-done.6.above_ref, ...), custom_call_target="tpu_custom_call" | custom-call | tf_op jit(solution)/shard_map/outer/pallas_call | solution.py:645
  (7 shorter events, 0.0 us)
Async XLA Ops:
  22.8 3.1 %collective-permute-start = (bf16[4,1040,128]{2,1,0:T(8,128)(2,1)S(1)}, bf16[4,1040,128]{2,1,0:T(8,128)(2,1)S(1)}, u32[]{:S(2)}, u32[]{:S(2)}) collective-permute-start(bf16[4,1040,128]{2,1,0:T(8,128)(2,1)S(1)} %get-tuple-element.19), channel_id=1, source_target_pairs={{0,32},{32,0},{64,96},{96,64},{128,160},{160,128},{192,224},{224,1... | collective-permute-start | bytes 3194888 | tf_op jit(solution)/shard_map/ppermute | solution.py:583
  25.8 5.1 %copy-start = (bf16[5,5,128,128]{3,2,1,0:T(8,128)(2,1)S(1)}, bf16[5,5,128,128]{3,2,1,0:T(8,128)(2,1)}, u32[]{:S(2)}) copy-start(bf16[5,5,128,128]{3,2,1,0:T(8,128)(2,1)} %param.26) | copy-start | bytes 2457604
  25.8 5.1 %copy-start.1 = (bf16[5,5,128,128]{3,2,1,0:T(8,128)(2,1)S(1)}, bf16[5,5,128,128]{3,2,1,0:T(8,128)(2,1)}, u32[]{:S(2)}) copy-start(bf16[5,5,128,128]{3,2,1,0:T(8,128)(2,1)} %param.28) | copy-start | bytes 2457604
  25.8 5.1 %copy-start.2 = (s32[8192]{0:T(1024)S(1)}, s32[8192]{0:T(1024)}, u32[]{:S(2)}) copy-start(s32[8192]{0:T(1024)} %param.19) | copy-start | bytes 98308
  26.6 7.8 %collective-permute-start.1 = (bf16[1040,128]{1,0:T(8,128)(2,1)S(1)}, bf16[1040,128]{1,0:T(8,128)(2,1)S(1)}, u32[]{:S(2)}, u32[]{:S(2)}) collective-permute-start(bf16[1040,128]{1,0:T(8,128)(2,1)S(1)} %get-tuple-element.21), channel_id=1, source_target_pairs={{0,64},{32,96},{64,128},{96,160},{128,192},{160,224},{192,0},{224,... | collective-permute-start | bytes 798728 | tf_op jit(solution)/shard_map/ppermute | solution.py:594
  28.2 8.9 %collective-permute-start.2 = (bf16[1040,128]{1,0:T(8,128)(2,1)S(1)}, bf16[1040,128]{1,0:T(8,128)(2,1)S(1)}, u32[]{:S(2)}, u32[]{:S(2)}) collective-permute-start(bf16[1040,128]{1,0:T(8,128)(2,1)S(1)} %get-tuple-element.22), channel_id=1, source_target_pairs={{0,128},{32,160},{64,192},{96,224},{128,0},{160,32},{192,64},{224,... | collective-permute-start | bytes 798728 | tf_op jit(solution)/shard_map/ppermute | solution.py:594
  29.0 13.3 %collective-permute-start.3 = (bf16[1040,128]{1,0:T(8,128)(2,1)S(1)}, bf16[1040,128]{1,0:T(8,128)(2,1)S(1)}, u32[]{:S(2)}, u32[]{:S(2)}) collective-permute-start(bf16[1040,128]{1,0:T(8,128)(2,1)S(1)} %get-tuple-element.23), channel_id=1, source_target_pairs={{0,192},{32,224},{64,0},{96,32},{128,64},{160,96},{192,128},{224,1... | collective-permute-start | bytes 798728 | tf_op jit(solution)/shard_map/ppermute | solution.py:594
  43.1 39.0 %copy-start.3 = (f32[128]{0:T(128)S(1)}, f32[128]{0:T(128)}, u32[]{:S(2)}) copy-start(f32[128]{0:T(128)} %param.27) | copy-start | bytes 1540
  65.9 7.1 %collective-permute-start.4 = (bf16[128,128]{1,0:T(8,128)(2,1)S(1)}, bf16[128,128]{1,0:T(8,128)(2,1)S(1)}, u32[]{:S(2)}, u32[]{:S(2)}) collective-permute-start(bf16[128,128]{1,0:T(8,128)(2,1)S(1)} %get-tuple-element.27), channel_id=1, source_target_pairs={{0,32},{32,64},{64,96},{96,128},{128,160},{160,192},{192,224},{1,3... | collective-permute-start | bytes 98312 | tf_op jit(solution)/shard_map/ppermute | solution.py:436
  71.0 5.2 %collective-permute-start.5 = (bf16[128,128]{1,0:T(8,128)(2,1)S(1)}, bf16[128,128]{1,0:T(8,128)(2,1)S(1)}, u32[]{:S(2)}, u32[]{:S(2)}) collective-permute-start(bf16[128,128]{1,0:T(8,128)(2,1)S(1)} %get-tuple-element.28), channel_id=1, source_target_pairs={{32,0},{64,32},{96,64},{128,96},{160,128},{192,160},{224,192},{33,... | collective-permute-start | bytes 98312 | tf_op jit(solution)/shard_map/ppermute | solution.py:436
  76.3 7.4 %collective-permute-start.6 = (bf16[320,128]{1,0:T(8,128)(2,1)S(1)}, bf16[320,128]{1,0:T(8,128)(2,1)S(1)}, u32[]{:S(2)}, u32[]{:S(2)}) collective-permute-start(bf16[320,128]{1,0:T(8,128)(2,1)S(1)} %bitcast.36), channel_id=1, source_target_pairs={{0,1},{1,2},{2,3},{3,4},{4,5},{5,6},{6,7},{7,8},{8,9},{9,10},{10,1... | collective-permute-start | bytes 245768 | tf_op jit(solution)/shard_map/ppermute | solution.py:436
  80.2 8.4 %copy-start.4 = (f32[128]{0:T(128)S(1)}, f32[128]{0:T(128)}, u32[]{:S(2)}) copy-start(f32[128]{0:T(128)} %param.29) | copy-start | bytes 1540
  80.2 8.3 %collective-permute-start.7 = (bf16[320,128]{1,0:T(8,128)(2,1)S(1)}, bf16[320,128]{1,0:T(8,128)(2,1)S(1)}, u32[]{:S(2)}, u32[]{:S(2)}) collective-permute-start(bf16[320,128]{1,0:T(8,128)(2,1)S(1)} %bitcast.37), channel_id=1, source_target_pairs={{1,0},{2,1},{3,2},{4,3},{5,4},{6,5},{7,6},{8,7},{9,8},{10,9},{11,1... | collective-permute-start | bytes 245768 | tf_op jit(solution)/shard_map/ppermute | solution.py:436

commit v4 on v3

--- a/solution.py
+++ b/solution.py
@@ -131,7 +131,7 @@
 
 def segment_kernel(
     live_smem,
-    enc_ref,
+    enc_hbm,
     gap_ref,
     pixel_ref,
     ids_ref,
@@ -144,6 +144,7 @@
     near_ref,
     far_ref,
     ray_ref,
+    encoded,
     spread,
     hidden,
     first_a,
@@ -158,13 +159,22 @@
     pos_ref,
     pos_smem,
     pos_sem,
+    enc_sems,
 ):
     step = pl.program_id(0)
+    rows = 2 * SUPER * SAMPLES
+
+    def load(n):
+        at = pl.ds(pl.multiple_of(n * rows, rows), rows)
+        return pltpu.make_async_copy(enc_hbm.at[at], encoded.at[at], enc_sems.at[n])
+
     to_smem = pltpu.make_async_copy(pos_ref, pos_smem, pos_sem)
     half = SUPER * SAMPLES // 2
 
     @pl.when(step == 0)
     def _():
+        for n in range(SLOTS // (2 * SUPER)):
+            load(n).start()
         zero = jnp.zeros((FEAT, FEAT), bf16)
         for wide, w in ((wide1, w1_ref), (wide2, w2_ref)):
             wide[:FEAT, :FEAT] = w[0]
@@ -183,8 +193,9 @@
     spread[pl.ds(start, chunk), :] = jnp.zeros((chunk, FEAT), f32)
 
     def layer_one(base, out):
+        at = pl.multiple_of(step * rows + base, half)
         x = jnp.concatenate(
-            [enc_ref[base : base + half, :], enc_ref[base + half : base + 2 * half, :]], axis=1
+            [encoded[pl.ds(at, half), :], encoded[pl.ds(at + half, half), :]], axis=1
         )
         out[...] = jnp.maximum((dot_nn(x, wide1[...]) + bias1).astype(bf16), 0.0)
 
@@ -199,6 +210,7 @@
                 lined = jnp.where(lane8 == s, total[SAMPLES * s : SAMPLES * (s + 1), :], lined)
             pre[2 * block + side] = lined
 
+    load(step).wait()
     layer_two(first_b, jnp.maximum(2 * step - 1, 0))
     layer_one(0, first_a)
     layer_two(first_a, 2 * step)
@@ -403,10 +415,11 @@
         grid_spec=pltpu.PrefetchScalarGridSpec(
             num_scalar_prefetch=1,
             grid=(SLOTS * SAMPLES // rows,),
-            in_specs=[pl.BlockSpec((rows, FEAT), lambda i, *_: (i, 0))]
+            in_specs=[pl.BlockSpec(memory_space=pltpu.HBM)]
             + [whole(a.shape) for a in (gaps, pixel, ids, w1, b1, w2, b2, wd, wf)],
             out_specs=[VMEM, VMEM, whole(pixel.shape)],
             scratch_shapes=[
+                pltpu.VMEM((SLOTS * SAMPLES, FEAT), bf16),
                 pltpu.VMEM((RAYS, FEAT), f32),
                 pltpu.VMEM((SLOTS * SAMPLES // 2, 2 * FEAT), bf16),
                 pltpu.VMEM((SUPER * SAMPLES // 2, 2 * FEAT), bf16),
@@ -421,6 +434,7 @@
                 pltpu.VMEM((SLOTS // LANES, LANES), i32),
                 pltpu.SMEM((SLOTS // LANES, LANES), i32),
                 pltpu.SemaphoreType.DMA,
+                pltpu.SemaphoreType.DMA((SLOTS // (2 * SUPER),)),
             ],
         ),
         out_shape=[out, out, shape_of(pixel.shape, i32)],

time: 92.5 us -> 90.4 us (0.977)
  Pallas kernels: 30.9 us -> 29 us
    pallas_call x1, Pallas kernels: 22.1 us -> 20.2 us  [segments(): pl.pallas_call(segment_kernel, grid_spec=pltpu.PrefetchScalarGridSpec(num...]
where the time goes in v4:
time: 90.4 us; the launch traced here: 90.2 us
  Pallas kernels  29 us (32%)
  blocking collectives  22 us (24%)
  waiting for transfers between devices  20.3 us (22%)
  starting transfers between devices  18 us (20%)
    all_to_all x1, blocking collectives, on_device(): lax.all_to_all(outgoing, 'rays', split_axis=0, concat_axis=0, tiled=True)  22 us
    pallas_call x1, Pallas kernels, segments(): pl.pallas_call(segment_kernel, grid_spec=pltpu.PrefetchScalarGridSpec(num...  20.2 us
    ppermute x4, starting transfers between devices, exchanged(): return (lax.ppermute(high, axis, up), lax.ppermute(low, axis, down))  12.9 us
    ppermute x3, waiting for transfers between devices, on_device(): lax.ppermute(pieces[k], 'depth', [(i, (i + 2 * k) % 8) for i in range(8)])  9.88 us
    ppermute x4, waiting for transfers between devices, exchanged(): return (lax.ppermute(high, axis, up), lax.ppermute(low, axis, down))  8.13 us
    ppermute x3, starting transfers between devices, on_device(): lax.ppermute(pieces[k], 'depth', [(i, (i + 2 * k) % 8) for i in range(8)])  4.34 us
    pallas_call x1, Pallas kernels, on_device(): pl.pallas_call(outer_kernel, in_specs=[VMEM] * 12, out_specs=VMEM, out_sh...  3.55 us
    ppermute x1, waiting for transfers between devices, on_device(): arrived = lax.ppermute(far, 'depth', [(i, i ^ 1) for i in range(8)])  2.31 us
  transfers between devices with their start and end apart: 8, of which 6 were waited for; matrix products, arithmetic and copies ran while one was open for 0% of the time, Pallas kernels for 3%

profile of v4, /device:TPU:15, one launch (start us, length us, event | category | flops | bytes accessed | tf_op | source)
XLA Modules:
  0.0 90.2 jit_solution(9412693725309123594)
XLA Ops:
  0.7 20.2 %segments.1 = (bf16[4,1040,128]{2,1,0:T(8,128)(2,1)S(1)}, bf16[4,1040,128]{2,1,0:T(8,128)(2,1)S(1)}, s32[64,128]{1,0:T(8,128)S(1)}) custom-call(s32[1]{0:T(128)} %bitcast.21.live_smem, bf16[40960,128]{1,0:T(8,128)(2,1)} %bitcast.32, f32[8,5120]{1,0:T(8,128)} %bitcast.35, s32[64,128]{1,0:T(8,128)} %bitcast.27, s32[40,128]{1,0:T(8,128)} %bitcast.38, ...), custom_call_target="tpu_custom_call" | custom-call | tf_op jit(solution)/shard_map/segments/pallas_call | solution.py:413
  20.8 0.8 collective-permute-start
  21.6 2.3 %collective-permute-done.arrived = bf16[4,1040,128]{2,1,0:T(8,128)(2,1)S(1)} collective-permute-done((bf16[4,1040,128]{2,1,0:T(8,128)(2,1)S(1)}, bf16[4,1040,128]{2,1,0:T(8,128)(2,1)S(1)}, u32[]{:S(2)}, u32[]{:S(2)}) %collective-permute-start) | collective-permute-done | bytes 1064992 | tf_op jit(solution)/shard_map/ppermute | solution.py:597
  23.9 0.0 copy-start
  23.9 0.8 pair.1
  24.7 1.5 %collective-permute-start.1 = (bf16[1040,128]{1,0:T(8,128)(2,1)S(1)}, bf16[1040,128]{1,0:T(8,128)(2,1)S(1)}, u32[]{:S(2)}, u32[]{:S(2)}) collective-permute-start(bf16[1040,128]{1,0:T(8,128)(2,1)S(1)} %get-tuple-element.21), channel_id=1, source_target_pairs={{0,64},{32,96},{64,128},{96,160},{128,192},{160,224},{192,0},{224,... | collective-permute-start | bytes 798728 | tf_op jit(solution)/shard_map/ppermute | solution.py:608
  26.3 0.8 collective-permute-start.2
  27.1 2.0 %collective-permute-start.3 = (bf16[1040,128]{1,0:T(8,128)(2,1)S(1)}, bf16[1040,128]{1,0:T(8,128)(2,1)S(1)}, u32[]{:S(2)}, u32[]{:S(2)}) collective-permute-start(bf16[1040,128]{1,0:T(8,128)(2,1)S(1)} %get-tuple-element.23), channel_id=1, source_target_pairs={{0,192},{32,224},{64,0},{96,32},{128,64},{160,96},{192,128},{224,1... | collective-permute-start | bytes 798728 | tf_op jit(solution)/shard_map/ppermute | solution.py:608
  29.1 0.0 copy-done
  29.1 0.0 copy-done.1
  29.1 0.0 copy-done.2
  29.1 1.5 %info.1 = (f32[4,16,128]{2,1,0:T(8,128)S(1)}, bf16[1280,256]{1,0:T(8,128)(2,1)S(1)}, bf16[1280,256]{1,0:T(8,128)(2,1)S(1)}) custom-call(s32[64,128]{1,0:T(8,128)S(1)} %bitcast.28, s32[64,128]{1,0:T(8,128)S(1)} %get-tuple-element.24.ray_ref, bf16[5,640,128]{2,1,0:T(8,128)(2,1)S(1)} %bitcast.22, bf16[5,640,128]{2,1,0:T(8,128)(2,1)S(1)} %bitcast.25), custom_call_target="tpu_custom_call" | custom-call | tf_op jit(solution)/shard_map/info/pallas_call | solution.py:613
  30.5 2.0 %collective-permute-done.1.p1_ref = bf16[1040,128]{1,0:T(8,128)(2,1)S(1)} collective-permute-done((bf16[1040,128]{1,0:T(8,128)(2,1)S(1)}, bf16[1040,128]{1,0:T(8,128)(2,1)S(1)}, u32[]{:S(2)}, u32[]{:S(2)}) %collective-permute-start.1) | collective-permute-done | bytes 266272 | tf_op jit(solution)/shard_map/ppermute | solution.py:608
  32.5 2.6 %collective-permute-done.2.p2_ref = bf16[1040,128]{1,0:T(8,128)(2,1)S(1)} collective-permute-done((bf16[1040,128]{1,0:T(8,128)(2,1)S(1)}, bf16[1040,128]{1,0:T(8,128)(2,1)S(1)}, u32[]{:S(2)}, u32[]{:S(2)}) %collective-permute-start.2) | collective-permute-done | bytes 266272 | tf_op jit(solution)/shard_map/ppermute | solution.py:608
  35.1 5.3 %collective-permute-done.3.p3_ref = bf16[1040,128]{1,0:T(8,128)(2,1)S(1)} collective-permute-done((bf16[1040,128]{1,0:T(8,128)(2,1)S(1)}, bf16[1040,128]{1,0:T(8,128)(2,1)S(1)}, u32[]{:S(2)}, u32[]{:S(2)}) %collective-permute-start.3) | collective-permute-done | bytes 266272 | tf_op jit(solution)/shard_map/ppermute | solution.py:608
  40.4 0.8 merge.1
  41.2 0.0 copy-start.3
  41.2 22.0 %all_to_all.5.in_ref = bf16[32,40,128]{2,1,0:T(8,128)(2,1)S(1)} all-to-all(bf16[32,40,128]{2,1,0:T(8,128)(2,1)S(1)} %merge.1), channel_id=1, replica_groups=mesh['depth'=8,'rays'=32] {'rays'}, dimensions={0} | all-to-all | bytes 655360 | tf_op jit(solution)/shard_map/all_to_all | solution.py:629
  63.3 0.7 place.1
  64.0 5.1 %collective-permute-start.4 = (bf16[128,128]{1,0:T(8,128)(2,1)S(1)}, bf16[128,128]{1,0:T(8,128)(2,1)S(1)}, u32[]{:S(2)}, u32[]{:S(2)}) collective-permute-start(bf16[128,128]{1,0:T(8,128)(2,1)S(1)} %get-tuple-element.27), channel_id=1, source_target_pairs={{0,32},{32,64},{64,96},{96,128},{128,160},{160,192},{192,224},{1,3... | collective-permute-start | bytes 98312 | tf_op jit(solution)/shard_map/ppermute | solution.py:450
  69.1 1.9 %collective-permute-start.5 = (bf16[128,128]{1,0:T(8,128)(2,1)S(1)}, bf16[128,128]{1,0:T(8,128)(2,1)S(1)}, u32[]{:S(2)}, u32[]{:S(2)}) collective-permute-start(bf16[128,128]{1,0:T(8,128)(2,1)S(1)} %get-tuple-element.28), channel_id=1, source_target_pairs={{32,0},{64,32},{96,64},{128,96},{160,128},{192,160},{224,192},{33,... | collective-permute-start | bytes 98312 | tf_op jit(solution)/shard_map/ppermute | solution.py:450
  71.0 0.0 collective-permute-done.4.left_ref
  71.1 3.3 %collective-permute-done.5.right_ref = bf16[128,128]{1,0:T(8,128)(2,1)S(1)} collective-permute-done((bf16[128,128]{1,0:T(8,128)(2,1)S(1)}, bf16[128,128]{1,0:T(8,128)(2,1)S(1)}, u32[]{:S(2)}, u32[]{:S(2)}) %collective-permute-start.5) | collective-permute-done | bytes 32800 | tf_op jit(solution)/shard_map/ppermute | solution.py:450
  74.3 3.9 %collective-permute-start.6 = (bf16[320,128]{1,0:T(8,128)(2,1)S(1)}, bf16[320,128]{1,0:T(8,128)(2,1)S(1)}, u32[]{:S(2)}, u32[]{:S(2)}) collective-permute-start(bf16[320,128]{1,0:T(8,128)(2,1)S(1)} %bitcast.36), channel_id=1, source_target_pairs={{0,1},{1,2},{2,3},{3,4},{4,5},{5,6},{6,7},{7,8},{8,9},{9,10},{10,1... | collective-permute-start | bytes 245768 | tf_op jit(solution)/shard_map/ppermute | solution.py:450
  78.3 0.0 copy-start.4
  78.3 1.9 %collective-permute-start.7 = (bf16[320,128]{1,0:T(8,128)(2,1)S(1)}, bf16[320,128]{1,0:T(8,128)(2,1)S(1)}, u32[]{:S(2)}, u32[]{:S(2)}) collective-permute-start(bf16[320,128]{1,0:T(8,128)(2,1)S(1)} %bitcast.37), channel_id=1, source_target_pairs={{1,0},{2,1},{3,2},{4,3},{5,4},{6,5},{7,6},{8,7},{9,8},{10,9},{11,1... | collective-permute-start | bytes 245768 | tf_op jit(solution)/shard_map/ppermute | solution.py:450
  80.2 0.0 copy-done.3
  80.2 1.5 %inner.1.inner_ref = bf16[960,128]{1,0:T(8,128)(2,1)S(1)} custom-call(bf16[1024,128]{1,0:T(8,128)(2,1)S(1)} %get-tuple-element.26.block_ref, bf16[128,128]{1,0:T(8,128)(2,1)S(1)} %collective-permute-done.4.left_ref, bf16[128,128]{1,0:T(8,128)(2,1)S(1)} %collective-permute-done.5.right_ref, bf16[1280,256]{1,0:T(8,128)(2,1)S(1)} %get-tuple-element.29.main_ref.main1_ref, ...), custom_call_target="tpu_custom_call" | custom-call | tf_op jit(solution)/shard_map/inner/pallas_call | solution.py:646
  81.7 0.0 collective-permute-done.6.above_ref
  81.7 4.9 %collective-permute-done.7.below_ref = bf16[320,128]{1,0:T(8,128)(2,1)S(1)} collective-permute-done((bf16[320,128]{1,0:T(8,128)(2,1)S(1)}, bf16[320,128]{1,0:T(8,128)(2,1)S(1)}, u32[]{:S(2)}, u32[]{:S(2)}) %collective-permute-start.7) | collective-permute-done | bytes 81952 | tf_op jit(solution)/shard_map/ppermute | solution.py:450
  86.6 0.0 copy-done.4
  86.6 3.6 %outer.1 = bf16[16,64,128]{2,1,0:T(8,128)(2,1)} custom-call(bf16[1024,128]{1,0:T(8,128)(2,1)S(1)} %get-tuple-element.26.block_ref, bf16[128,128]{1,0:T(8,128)(2,1)S(1)} %collective-permute-done.4.left_ref, bf16[128,128]{1,0:T(8,128)(2,1)S(1)} %collective-permute-done.5.right_ref, bf16[320,128]{1,0:T(8,128)(2,1)S(1)} %collective-permute-done.6.above_ref, ...), custom_call_target="tpu_custom_call" | custom-call | tf_op jit(solution)/shard_map/outer/pallas_call | solution.py:659
  (7 shorter events, 0.0 us)
Async XLA Ops:
  20.8 3.1 %collective-permute-start = (bf16[4,1040,128]{2,1,0:T(8,128)(2,1)S(1)}, bf16[4,1040,128]{2,1,0:T(8,128)(2,1)S(1)}, u32[]{:S(2)}, u32[]{:S(2)}) collective-permute-start(bf16[4,1040,128]{2,1,0:T(8,128)(2,1)S(1)} %get-tuple-element.19), channel_id=1, source_target_pairs={{0,32},{32,0},{64,96},{96,64},{128,160},{160,128},{192,224},{224,1... | collective-permute-start | bytes 3194888 | tf_op jit(solution)/shard_map/ppermute | solution.py:597
  23.9 5.1 %copy-start = (bf16[5,5,128,128]{3,2,1,0:T(8,128)(2,1)S(1)}, bf16[5,5,128,128]{3,2,1,0:T(8,128)(2,1)}, u32[]{:S(2)}) copy-start(bf16[5,5,128,128]{3,2,1,0:T(8,128)(2,1)} %param.26) | copy-start | bytes 2457604
  23.9 5.1 %copy-start.1 = (bf16[5,5,128,128]{3,2,1,0:T(8,128)(2,1)S(1)}, bf16[5,5,128,128]{3,2,1,0:T(8,128)(2,1)}, u32[]{:S(2)}) copy-start(bf16[5,5,128,128]{3,2,1,0:T(8,128)(2,1)} %param.28) | copy-start | bytes 2457604
  23.9 5.1 %copy-start.2 = (s32[8192]{0:T(1024)S(1)}, s32[8192]{0:T(1024)}, u32[]{:S(2)}) copy-start(s32[8192]{0:T(1024)} %param.19) | copy-start | bytes 98308
  24.7 7.8 %collective-permute-start.1 = (bf16[1040,128]{1,0:T(8,128)(2,1)S(1)}, bf16[1040,128]{1,0:T(8,128)(2,1)S(1)}, u32[]{:S(2)}, u32[]{:S(2)}) collective-permute-start(bf16[1040,128]{1,0:T(8,128)(2,1)S(1)} %get-tuple-element.21), channel_id=1, source_target_pairs={{0,64},{32,96},{64,128},{96,160},{128,192},{160,224},{192,0},{224,... | collective-permute-start | bytes 798728 | tf_op jit(solution)/shard_map/ppermute | solution.py:608
  26.3 8.9 %collective-permute-start.2 = (bf16[1040,128]{1,0:T(8,128)(2,1)S(1)}, bf16[1040,128]{1,0:T(8,128)(2,1)S(1)}, u32[]{:S(2)}, u32[]{:S(2)}) collective-permute-start(bf16[1040,128]{1,0:T(8,128)(2,1)S(1)} %get-tuple-element.22), channel_id=1, source_target_pairs={{0,128},{32,160},{64,192},{96,224},{128,0},{160,32},{192,64},{224,... | collective-permute-start | bytes 798728 | tf_op jit(solution)/shard_map/ppermute | solution.py:608
  27.1 13.3 %collective-permute-start.3 = (bf16[1040,128]{1,0:T(8,128)(2,1)S(1)}, bf16[1040,128]{1,0:T(8,128)(2,1)S(1)}, u32[]{:S(2)}, u32[]{:S(2)}) collective-permute-start(bf16[1040,128]{1,0:T(8,128)(2,1)S(1)} %get-tuple-element.23), channel_id=1, source_target_pairs={{0,192},{32,224},{64,0},{96,32},{128,64},{160,96},{192,128},{224,1... | collective-permute-start | bytes 798728 | tf_op jit(solution)/shard_map/ppermute | solution.py:608
  41.2 39.0 %copy-start.3 = (f32[128]{0:T(128)S(1)}, f32[128]{0:T(128)}, u32[]{:S(2)}) copy-start(f32[128]{0:T(128)} %param.27) | copy-start | bytes 1540
  64.0 7.1 %collective-permute-start.4 = (bf16[128,128]{1,0:T(8,128)(2,1)S(1)}, bf16[128,128]{1,0:T(8,128)(2,1)S(1)}, u32[]{:S(2)}, u32[]{:S(2)}) collective-permute-start(bf16[128,128]{1,0:T(8,128)(2,1)S(1)} %get-tuple-element.27), channel_id=1, source_target_pairs={{0,32},{32,64},{64,96},{96,128},{128,160},{160,192},{192,224},{1,3... | collective-permute-start | bytes 98312 | tf_op jit(solution)/shard_map/ppermute | solution.py:450
  69.1 5.2 %collective-permute-start.5 = (bf16[128,128]{1,0:T(8,128)(2,1)S(1)}, bf16[128,128]{1,0:T(8,128)(2,1)S(1)}, u32[]{:S(2)}, u32[]{:S(2)}) collective-permute-start(bf16[128,128]{1,0:T(8,128)(2,1)S(1)} %get-tuple-element.28), channel_id=1, source_target_pairs={{32,0},{64,32},{96,64},{128,96},{160,128},{192,160},{224,192},{33,... | collective-permute-start | bytes 98312 | tf_op jit(solution)/shard_map/ppermute | solution.py:450
  74.3 7.4 %collective-permute-start.6 = (bf16[320,128]{1,0:T(8,128)(2,1)S(1)}, bf16[320,128]{1,0:T(8,128)(2,1)S(1)}, u32[]{:S(2)}, u32[]{:S(2)}) collective-permute-start(bf16[320,128]{1,0:T(8,128)(2,1)S(1)} %bitcast.36), channel_id=1, source_target_pairs={{0,1},{1,2},{2,3},{3,4},{4,5},{5,6},{6,7},{7,8},{8,9},{9,10},{10,1... | collective-permute-start | bytes 245768 | tf_op jit(solution)/shard_map/ppermute | solution.py:450
  78.3 8.3 %copy-start.4 = (f32[128]{0:T(128)S(1)}, f32[128]{0:T(128)}, u32[]{:S(2)}) copy-start(f32[128]{0:T(128)} %param.29) | copy-start | bytes 1540
  78.3 8.3 %collective-permute-start.7 = (bf16[320,128]{1,0:T(8,128)(2,1)S(1)}, bf16[320,128]{1,0:T(8,128)(2,1)S(1)}, u32[]{:S(2)}, u32[]{:S(2)}) collective-permute-start(bf16[320,128]{1,0:T(8,128)(2,1)S(1)} %bitcast.37), channel_id=1, source_target_pairs={{1,0},{2,1},{3,2},{4,3},{5,4},{6,5},{7,6},{8,7},{9,8},{10,9},{11,1... | collective-permute-start | bytes 245768 | tf_op jit(solution)/shard_map/ppermute | solution.py:450
